TPU v7x, 128 devices: a whole 4x4x4 slice. The times are simulated.
128 devices in a mesh: dp: 16 (over x, y), expert: 8 (over z, core).
Axes of the slice: x: 4, y: 4, z: 4, core: 2. Of those that a mesh axis runs over, the one named last changes fastest.
Arguments:
- tokens: bfloat16 [2048, 6144], P('dp'), may hold values from -6 to 6
- routes: int32 [2048, 2], P('dp'), may hold values from 0 to 7, all different within a row; in each aligned block of 128 rows (0 to 127, 128 to 255, ...) at most 64 rows name the same one
- gates: float32 [2048, 2], P('dp'), may hold values from 0.1 to 1
- capacity: int32 [8], replicated, may hold values from 32 to 64, as said below
- w_gate: bfloat16 [8, 6144, 8192], P('expert', None, 'dp'), may hold values from -0.078125 to 0.078125
- w_up: bfloat16 [8, 6144, 8192], P('expert', None, 'dp'), may hold values from -0.078125 to 0.078125
- w_down: bfloat16 [8, 8192, 6144], P('expert', 'dp'), may hold values from -0.0625 to 0.0625
Outputs:
- mixed: bfloat16 [2048, 6144], P('dp', 'expert')
Inputs may be any that keep to these rules, and one draw needn't show every extreme that they name: `routes`: each token names two different experts. Within the 128 tokens of one index of dp no expert is named by more than 64 tokens, and in some shards one expert is named by exactly 64. Some expert's capacity is exactly 64.
All inputs are finite; a program needn't handle non-finite values.
Results may differ from a plain program's by a relative error of at most 0.015.
Values may be sent and summed in bfloat16 or wider, within the bound.
No kernel may reach another device: no remote copies, remote signals or barrier semaphores. Data moves between devices by JAX's collectives and lax.ppermute only.
A program may use at most 128 MiB of HBM per device.

v0:
```python
import jax
import jax.numpy as jnp
from jax import lax
from jax.sharding import PartitionSpec as P


def on_device(tokens, routes, gates, capacity, w_gate, w_up, w_down):
    owner_index = lax.axis_index("expert")
    group_size = lax.axis_size("expert")
    local_rows = tokens.shape[0]
    num_experts = group_size * w_gate.shape[0]
    slot_count = 4 * local_rows // num_experts
    matched = routes == owner_index
    member = jnp.any(matched, axis=-1).astype(jnp.int32)
    weight = jnp.sum(jnp.where(matched, gates, 0.0), axis=-1)
    position = jnp.cumsum(member) - member
    limit_value = jnp.sum(
        jnp.where(jnp.arange(num_experts, dtype=jnp.int32) == owner_index, capacity, 0)
    )
    retained = (member == 1) & (position < limit_value)
    slot_ids = jnp.arange(slot_count, dtype=jnp.int32)
    selector = (retained[None, :] & (position[None, :] == slot_ids[:, None])).astype(jnp.bfloat16)
    slot_rows = jnp.dot(selector, tokens, preferred_element_type=jnp.float32).astype(jnp.bfloat16)
    gate_panel = w_gate[0]
    up_panel = w_up[0]
    down_panel = w_down[0]
    block_rows = lax.all_gather(slot_rows, "dp", axis=0, tiled=True)
    gate_value = jnp.dot(block_rows, gate_panel, preferred_element_type=jnp.float32)
    up_value = jnp.dot(block_rows, up_panel, preferred_element_type=jnp.float32)
    hidden = (jax.nn.silu(gate_value) * up_value).astype(jnp.bfloat16)
    partial_value = jnp.dot(hidden, down_panel, preferred_element_type=jnp.float32)
    returned = lax.psum_scatter(
        partial_value.astype(jnp.bfloat16), "dp", scatter_dimension=0, tiled=True
    ).astype(jnp.float32)
    placed = jnp.einsum(
        "ct,cd->td", selector.astype(jnp.float32), returned, precision=lax.Precision.HIGHEST
    )
    weighted = weight[:, None] * placed
    summed = lax.psum(weighted.astype(jnp.bfloat16), "expert").astype(jnp.float32)
    feature_width = summed.shape[1] // group_size
    result = lax.dynamic_slice_in_dim(summed, owner_index * feature_width, feature_width, 1)
    return result.astype(jnp.bfloat16)


def solution(mesh):
    in_specs = (
        P("dp", None),
        P("dp", None),
        P("dp", None),
        P(),
        P("expert", None, "dp"),
        P("expert", None, "dp"),
        P("expert", "dp", None),
    )
    out_specs = P("dp", "expert")
    return jax.shard_map(
        on_device, mesh=mesh, in_specs=in_specs, out_specs=out_specs, check_vma=False
    )
```

profile of v0, /device:TPU:0, one launch (start us, length us, event | category | flops | bytes accessed | tf_op | source)
XLA Modules:
  0.0 303.3 jit_solution(16822140769576966833)
XLA Ops:
  6.5 0.0 copy-start
  6.5 0.0 all-gather.2.cloned.1.call-start
  6.5 0.8 fusion.16
  7.4 0.1 copy.9
  7.5 0.2 reduce-window.7
  7.7 0.1 reduce
  7.8 1.3 fusion.15
  9.1 0.7 compare_and_fusion
  9.7 0.0 copy-done
  9.7 1.3 convolution_convert_fusion.1
  11.0 0.0 all-gather.2.cloned.1.call-update
  11.0 0.0 reduce-scatter.2.cloned.1.call-start
  11.1 92.2 %all-gather.2.cloned.1.call-done = bf16[1024,6144]{1,0:T(8,128)(2,1)} async-done(((bf16[64,6144]{1,0:T(8,128)(2,1)}), bf16[1024,6144]{1,0:T(8,128)(2,1)}) %all-gather.2.cloned.1.call-update) | async-done | bytes 12582928 | tf_op jit(solution)/shard_map/all_gather | solution.py:27
  103.3 0.0 copy-start.3
  103.3 11.6 %fusion.2 = f32[1024,512]{1,0:T(8,128)S(1)} fusion(bf16[1024,6144]{1,0:T(8,128)(2,1)} %all-gather.2.cloned.1.call-done, bf16[1,6144,512]{2,1,0:T(8,128)(2,1)} %param.12), kind=kOutput, calls=%fused_computation.5 | convolution fusion | flops 6442450944 | bytes 20971520 | tf_op jit(solution)/shard_map/dot_general | solution.py:29
  114.9 0.0 copy-done.3
  114.9 0.0 copy-start.4
  114.9 9.0 %multiply_convert_fusion = bf16[1024,512]{1,0:T(8,128)(2,1)S(1)} fusion(f32[1024,512]{1,0:T(8,128)S(1)} %fusion.2, bf16[1024,6144]{1,0:T(8,128)(2,1)S(1)} %copy-done.3, bf16[1,6144,512]{2,1,0:T(8,128)(2,1)} %param.11), kind=kOutput, calls=%fused_computation.9 | convolution fusion | flops 6445596672 | bytes 22020096 | tf_op jit(solution)/shard_map/dot_general | solution.py:28
  124.0 0.0 copy-done.4
  124.0 9.6 %convolution_convert_fusion = bf16[1024,6144]{1,0:T(8,128)(2,1)} fusion(bf16[1024,512]{1,0:T(8,128)(2,1)S(1)} %multiply_convert_fusion, bf16[1,512,6144]{2,1,0:T(8,128)(2,1)S(1)} %copy-done.4), kind=kOutput, calls=%fused_computation | convolution fusion | flops 6448742400 | bytes 19922944 | tf_op jit(solution)/shard_map/dot_general | solution.py:31
  133.6 0.0 copy-start.1
  133.6 0.0 copy-start.2
  133.6 0.0 reduce-scatter.2.cloned.1.call-update
  133.6 0.0 all-reduce.2.cloned.1.call-start
  133.6 0.6 copy-done.1
  134.2 0.0 copy-done.2
  134.3 94.4 %reduce-scatter.2.cloned.1.call-done = bf16[64,6144]{1,0:T(8,128)(2,1)} async-done(((bf16[1024,6144]{1,0:T(8,128)(2,1)}), bf16[64,6144]{1,0:T(8,128)(2,1)}) %reduce-scatter.2.cloned.1.call-update) | async-done | bytes 786448 | tf_op jit(solution)/shard_map/reduce_scatter | solution.py:32
  228.7 2.9 fusion
  231.6 0.0 all-reduce.2.cloned.1.call-update
  231.6 63.5 %all-reduce.2.cloned.1.call-done = bf16[128,6144]{1,0:T(8,128)(2,1)} async-done(((bf16[128,6144]{1,0:T(8,128)(2,1)}), bf16[128,6144]{1,0:T(8,128)(2,1)}) %all-reduce.2.cloned.1.call-update) | async-done | bytes 1572880 | tf_op jit(solution)/shard_map/psum | solution.py:39
  295.1 1.6 convert_convert_fusion
  (3 shorter events, 0.0 us)
Async XLA Ops:
  6.5 3.2 %copy-start = (bf16[128,6144]{1,0:T(8,128)(2,1)S(1)}, bf16[128,6144]{1,0:T(8,128)(2,1)}, u32[]{:S(2)}) copy-start(bf16[128,6144]{1,0:T(8,128)(2,1)} %param.7) | copy-start | bytes 4718596
  6.5 96.8 %all-gather.2.cloned.1.call-start = ((), (), s32[]{:S(2)}) async-start(), calls=%async_computation.1 | async-start | bytes 13369344 | tf_op jit(solution)/shard_map/all_gather | solution.py:27
  11.0 217.6 %reduce-scatter.2.cloned.1.call-start = ((), (), s32[]{:S(2)}) async-start(), calls=%async_computation.2 | async-start | bytes 13369344 | tf_op jit(solution)/shard_map/reduce_scatter | solution.py:32
  103.3 11.6 %copy-start.3 = (bf16[1024,6144]{1,0:T(8,128)(2,1)S(1)}, bf16[1024,6144]{1,0:T(8,128)(2,1)}, u32[]{:S(2)}) copy-start(bf16[1024,6144]{1,0:T(8,128)(2,1)} %all-gather.2.cloned.1.call-done) | copy-start | bytes 37748740
  114.9 9.1 %copy-start.4 = (bf16[1,512,6144]{2,1,0:T(8,128)(2,1)S(1)}, bf16[1,512,6144]{2,1,0:T(8,128)(2,1)}, u32[]{:S(2)}) copy-start(bf16[1,512,6144]{2,1,0:T(8,128)(2,1)} %param.13) | copy-start | bytes 18874372
  133.6 0.7 copy-start.1
  133.6 0.7 copy-start.2
  133.6 161.5 %all-reduce.2.cloned.1.call-start = ((), (), s32[]{:S(2)}) async-start(), calls=%async_computation.3 | async-start | bytes 3145728 | tf_op jit(solution)/shard_map/psum | solution.py:39
Sparse Core Ops, SparseCore 0:
  11.2 92.1 all-gather.1
  133.7 94.9 reduce-scatter.1
  231.7 63.3 all-reduce.1
where the time goes:
time: 304 us; the launch traced here: 303 us
  waiting for transfers between devices  250 us (82%)
  matrix products  34.4 us (11%)
  between operations  13.2 us (4%)
  other arithmetic  4.69 us (2%)
    reduce_scatter x1, waiting for transfers between devices, on_device(): lax.psum_scatter(partial_value.astype(jnp.bfloat16), 'dp', scatter_dimens...  94.4 us
    all_gather x1, waiting for transfers between devices, on_device(): block_rows = lax.all_gather(slot_rows, 'dp', axis=0, tiled=True)  92.2 us
    psum x1, waiting for transfers between devices, on_device(): lax.psum(weighted.astype(jnp.bfloat16), 'expert').astype(jnp.float32)  63.5 us
    dot_general x1, matrix products, on_device(): up_value = jnp.dot(block_rows, up_panel, preferred_element_type=jnp.float32)  11.6 us
    dot_general x1, matrix products, on_device(): jnp.dot(hidden, down_panel, preferred_element_type=jnp.float32)  9.56 us
    dot_general x1, matrix products, on_device(): jnp.dot(block_rows, gate_panel, preferred_element_type=jnp.float32)  9.04 us
  transfers between devices with their start and end apart: 3, of which 3 were waited for; matrix products, arithmetic and copies ran while one was open for 0% of the time, Pallas kernels for 0%

commit v1 on v0

v1 whole, which is shorter than its diff:
```python
import jax
import jax.numpy as jnp
from jax import lax
from jax.experimental import pallas as pl
from jax.experimental.pallas import tpu as pltpu
from jax.sharding import PartitionSpec as P


SIDE = 4
CORES = 2
F32 = jnp.float32
BF16 = jnp.bfloat16
STEPS = 4


def move(value, route):
    pairs = []
    for device in range(SIDE * SIDE * SIDE * CORES):
        rest, core = divmod(device, CORES)
        rest, z = divmod(rest, SIDE)
        x, y = divmod(rest, SIDE)
        x, y, z, core = route(x, y, z, core)
        pairs.append((device, ((x % SIDE * SIDE + y % SIDE) * SIDE + z % SIDE) * CORES + core))
    return lax.ppermute(value, ("dp", "expert"), pairs)


def hop(value, leg, step):
    def route(x, y, z, core):
        if core == leg:
            return x + step, y, z, core
        return x, y + step, z, core

    return move(value, route)


def hop_z(value, step):
    return move(value, lambda x, y, z, core: (x, y, z + step, core))


def swap(value):
    return move(value, lambda x, y, z, core: (x, y, z, 1 - core))


def ring_gather(block, leg):
    half = block.shape[0] // 2
    before = hop(block, leg, 1)
    after = hop(block, leg, -1)
    far_low = hop(before[:half], leg, 1)
    far_high = hop(after[half:], leg, -1)
    return before, after, far_low, far_high


def add(first, *others):
    total = first.astype(F32)
    for other in others:
        total = total + other.astype(F32)
    return total


def ring_scatter(own, before, after, far, leg):
    low_after = hop(before[1], leg, -1)
    low_before = hop(after[0], leg, 1)
    low = hop(far[0], leg, -1)
    high = hop(far[1], leg, 1)
    from_after = hop(add(before[0], low).astype(BF16), leg, -1)
    from_before = hop(add(after[1], high).astype(BF16), leg, 1)
    return own[0], low_before, from_after, own[1], low_after, from_before


def vmem_call(kernel, outs, *args, scalars=0, blocks=0, limit=20):
    specs = [pl.BlockSpec(memory_space=pltpu.SMEM)] * scalars
    specs += [pl.BlockSpec(memory_space=pltpu.VMEM)] * (len(args) - scalars - blocks)
    specs += [pl.BlockSpec()] * blocks
    space = pl.BlockSpec(memory_space=pltpu.VMEM) if limit < 50 else pl.BlockSpec()
    return pl.pallas_call(
        kernel,
        in_specs=specs,
        out_specs=[space] * len(outs),
        out_shape=[jax.ShapeDtypeStruct(shape, dtype) for shape, dtype in outs],
        compiler_params=pltpu.CompilerParams(vmem_limit_bytes=limit * 2**20),
    )(*args)


def line_kernel(*refs):
    chains, (minus, plus, near_minus, near_plus, own) = (refs[:6], refs[6:12]), refs[12:]
    tile = 512
    q = near_minus.shape[0] // 2

    @pl.loop(0, minus.shape[1] // tile)
    def _(i):
        at = pl.ds(pl.multiple_of(i * tile, tile), tile)
        for k, (own_low, low_before, from_after, own_high, low_after, from_before) in enumerate(chains):
            low = add(own_low[:, at], low_before[:, at], from_after[:, at])
            high = add(own_high[:, at], low_after[:, at], from_before[:, at])

            def put(out, row, value):
                out[pl.ds(row + k * q, q), at] = value.astype(out.dtype)

            put(own, 0, low[:q])
            put(own, 2 * q, low[q:2 * q])
            put(near_minus, 0, low[2 * q:3 * q])
            put(minus, 2 * q, low[3 * q:])
            put(plus, 2 * q, high[:q])
            put(near_plus, 0, high[q:2 * q])
            put(minus, 0, high[2 * q:3 * q])
            put(plus, 0, high[3 * q:])


def sum_kernel(place, own, from_minus, from_plus, near_after, near_before, mine, theirs):
    half = near_after.shape[0]
    q = half // 2
    width = mine.shape[1] // SIDE

    @pl.loop(0, SIDE)
    def _(k):
        to = pl.ds(pl.multiple_of(k * width, width), width)
        for core, out in ((place[1], mine), (1 - place[1], theirs)):
            at = pl.ds(pl.multiple_of((CORES * k + core) * width, width), width)
            first = add(own[:half, at], from_plus[half:, at], near_after[:, at]).astype(BF16)
            second = add(own[half:, at], from_minus[half:, at], near_before[:, at]).astype(BF16)
            out[:, to] = jnp.concatenate([first[:q], second[:q], first[q:], second[q:]], 0)


def spread_kernel(place, mine, theirs, picks, weights, *outs):
    half = mine.shape[0] // 2
    width = outs[0].shape[1]
    for step, out in enumerate(outs):
        at = pl.ds(pl.multiple_of((place[0] + step) % SIDE * width, width), width)
        total = 0.0
        for e in range(2):
            rows = [mine[e * half:(e + 1) * half, at], theirs[(1 - e) * half:(2 - e) * half, at]]
            value = jnp.dot(picks[e], jnp.concatenate(rows, 0), preferred_element_type=F32)
            total = total + weights[:, e:e + 1] * value
        out[...] = total.astype(out.dtype)


def final_kernel(own, *refs):
    refs[-1][...] = add(own[...], *[ref[...] for ref in refs[:-1]]).astype(BF16)


def ffn_kernel(n, *refs):
    pieces, (w_gate, w_up, w_down) = refs[:n], refs[n:n + 3]
    outs, (gate_sum, up_sum, hidden) = refs[n + 3:-3], refs[-3:]
    i = pl.program_id(0)

    @pl.when(i < STEPS)
    def _():
        block = jnp.concatenate([piece[...] for piece in pieces], 0)
        tile = block.shape[1]
        at = pl.ds(pl.multiple_of(i * tile, tile), tile)
        gate_value = jnp.dot(block, w_gate[0, at], preferred_element_type=F32)
        up_value = jnp.dot(block, w_up[0, at], preferred_element_type=F32)

        @pl.when(i == 0)
        def _():
            gate_sum[...] = gate_value
            up_sum[...] = up_value

        @pl.when(i > 0)
        def _():
            gate_sum[...] += gate_value
            up_sum[...] += up_value

        @pl.when(i == STEPS - 1)
        def _():
            hidden[...] = (jax.nn.silu(gate_sum[...]) * up_sum[...]).astype(BF16)

    @pl.when(i >= STEPS)
    def _():
        tile = outs[0].shape[1]
        cols = pl.ds(pl.multiple_of((i - STEPS) * tile, tile), tile)
        value = jnp.dot(hidden[...], w_down[0, :, cols], preferred_element_type=F32).astype(BF16)
        at = 0
        for out in outs:
            out[...] = value[at:at + out.shape[0]]
            at += out.shape[0]


def ffn(pieces, out_rows, w_gate, w_up, w_down):
    width, inner = w_gate.shape[1:]
    sizes = [piece.shape[0] for piece in pieces]
    rows = sum(sizes)
    outs = rows // out_rows
    tile = width // STEPS

    def first(i):
        return jnp.minimum(i, STEPS - 1)

    def second(i):
        return jnp.maximum(i - STEPS, 0)

    return pl.pallas_call(
        lambda *refs: ffn_kernel(len(sizes), *refs),
        name="ffn",
        grid=(2 * STEPS,),
        in_specs=[pl.BlockSpec((size, tile), lambda i: (0, first(i))) for size in sizes]
        + [pl.BlockSpec(memory_space=pltpu.VMEM)] * 3,
        out_specs=[pl.BlockSpec((out_rows, tile), lambda i: (0, second(i)))] * outs,
        out_shape=[jax.ShapeDtypeStruct((out_rows, width), BF16)] * outs,
        scratch_shapes=[
            pltpu.VMEM((rows, inner), F32),
            pltpu.VMEM((rows, inner), F32),
            pltpu.VMEM((rows, inner), BF16),
        ],
        cost_estimate=pl.CostEstimate(
            flops=6 * rows * width * inner,
            bytes_accessed=6 * width * inner + 4 * rows * width,
            transcendentals=rows * inner,
        ),
        compiler_params=pltpu.CompilerParams(vmem_limit_bytes=20 * 2**20),
    )(*pieces, w_gate, w_up, w_down)


def layer(tokens, routes, gates, capacity, w_gate, w_up, w_down):
    owner = lax.axis_index("expert")
    rows = tokens.shape[0]
    experts = lax.axis_size("expert")
    slots = 4 * rows // experts
    half = slots // CORES
    core = owner % CORES
    z = owner // CORES
    slot_ids = (core * half + jnp.arange(slots, dtype=jnp.int32)) % slots

    def route(expert):
        matched = routes == expert
        member = jnp.any(matched, axis=-1).astype(jnp.int32)
        weight = jnp.sum(jnp.where(matched, gates, 0.0), axis=-1)
        position = jnp.cumsum(member) - member
        limit = jnp.sum(jnp.where(jnp.arange(experts, dtype=jnp.int32) == expert, capacity, 0))
        kept = (member == 1) & (position < limit)
        picked = kept[None, :] & (position[None, :] == slot_ids[:, None])
        return picked.astype(BF16), weight

    pick_other, weight_other = route(owner + 1 - 2 * core)
    pick_own, weight_own = route(owner)
    block = jnp.dot(
        jnp.concatenate([pick_other[:half], pick_own[:half]], 0), tokens, preferred_element_type=F32
    ).astype(BF16)

    def gather(block):
        near = ring_gather(block, 0)
        line = jnp.concatenate((block,) + near, 0)
        return (line,) + ring_gather(line, 1)

    other = gather(block[:half])
    own = gather(block[half:])
    given = [swap(value) for value in other]
    weights = (w_gate, w_up, w_down)
    q = other[3].shape[0]
    line = ffn([own[0], given[0]], q, *weights)
    near_given = ffn([given[1], given[2]], q, *weights)
    near_own = ffn([own[1], own[2]], q, *weights)
    far = ffn([own[3], own[4], given[3], given[4]], q, *weights)
    back = {}
    for name, values in (("pl", line[2:]), ("pn", near_given), ("pf", far[2:])):
        back[name] = [swap(value) for value in values]

    def scatter(line, near, far):
        return ring_scatter(line, near[:2], near[2:], far, 1)

    width = tokens.shape[1]
    q = half // 2
    minus, plus, near_minus, near_plus, own_sum = vmem_call(
        line_kernel,
        [((4 * q, width), BF16)] * 2 + [((2 * q, width), F32)] * 2 + [((4 * q, width), F32)],
        *scatter(back["pl"], back["pn"], back["pf"]),
        *scatter(line[:2], near_own, far[:2]),
    )
    from_minus = hop(minus, 0, -1)
    from_plus = hop(plus, 0, 1)
    near_after = hop(add(near_minus, from_minus[:2 * q]).astype(BF16), 0, -1)
    near_before = hop(add(near_plus, from_plus[:2 * q]).astype(BF16), 0, 1)

    part = width // experts
    picks = jnp.stack([pick_other.T, pick_own.T])
    weights = jnp.stack([weight_other, weight_own], 1)
    place = jnp.stack([z, core])
    mine, theirs = vmem_call(
        sum_kernel,
        [((slots, SIDE * part), BF16)] * 2,
        place, own_sum, from_minus, from_plus, near_after, near_before,
        scalars=1,
    )
    sums = vmem_call(
        spread_kernel,
        [((rows, part), F32)] + [((rows, part), BF16)] * (SIDE - 1),
        place, mine, swap(theirs), picks, weights,
        scalars=1,
    )
    came = [hop_z(sums[step], step if step < 3 else -1) for step in (2, 1, 3)]
    return vmem_call(final_kernel, [((rows, part), BF16)], sums[0], *came)[0]


def solution(mesh):
    in_specs = (
        P("dp", None),
        P("dp", None),
        P("dp", None),
        P(),
        P("expert", None, "dp"),
        P("expert", None, "dp"),
        P("expert", "dp", None),
    )
    return jax.shard_map(layer, mesh=mesh, in_specs=in_specs, out_specs=P("dp", "expert"), check_vma=False)
```

time: 304 us -> 242 us (0.80)
  waiting for transfers between devices: 250 us -> 134 us
  starting transfers between devices: 0.09 us -> 57 us
  Pallas kernels: 0 us -> 35.1 us
  matrix products: 34.4 us -> 0.36 us
  between operations: 13.2 us -> 0.46 us
  local copies, waits for them, and re-layouts: 0.75 us -> 9.05 us
    ppermute x0 -> x49, waiting for transfers between devices: none -> 134 us  [move(): return lax.ppermute(value, ('dp', 'expert'), pairs)]
    reduce_scatter x1 -> x0, waiting for transfers between devices: 94.4 us -> none  [on_device(): lax.psum_scatter(partial_value.astype(jnp.bfloat16), 'dp', scatter_dimens...]
    all_gather x1 -> x0, waiting for transfers between devices: 92.2 us -> none  [on_device(): block_rows = lax.all_gather(slot_rows, 'dp', axis=0, tiled=True)]
    psum x1 -> x0, waiting for transfers between devices: 63.5 us -> none  [on_device(): lax.psum(weighted.astype(jnp.bfloat16), 'expert').astype(jnp.float32)]
    ppermute x0 -> x49, starting transfers between devices: none -> 57 us  [move(): return lax.ppermute(value, ('dp', 'expert'), pairs)]
    pallas_call x0 -> x8, Pallas kernels: none -> 35.1 us  [the longest x4 30.4 us: ffn(): pl.pallas_call(lambda *refs: ffn_kernel(len(sizes), *refs), name='ffn', g...]
    dot_general x5 -> x1, matrix products: 34.4 us -> 0.36 us  [layer(): jnp.dot(jnp.concatenate([pick_other[:half], pick_own[:half]], 0), tokens,...]
    unnamed x10 -> x38, local copies, waits for them, and re-layouts: 0.63 us -> 8.27 us
  transfers between devices with their start and end apart: 3 -> 49, of which waited for: 3 -> 24; matrix products, arithmetic and copies ran while one was open for 0% -> 1% of each run, Pallas kernels for 0% -> 13%
where the time goes in v1:
time: 242 us
  waiting for transfers between devices  134 us (55%)
  starting transfers between devices  57 us (24%)
  Pallas kernels  35.1 us (15%)
  local copies, waits for them, and re-layouts  9.05 us (4%)
  other arithmetic  5.72 us (2%)
    ppermute x49, waiting for transfers between devices, move(): return lax.ppermute(value, ('dp', 'expert'), pairs)  134 us
    ppermute x49, starting transfers between devices, move(): return lax.ppermute(value, ('dp', 'expert'), pairs)  57 us
    pallas_call x4, Pallas kernels, ffn(): pl.pallas_call(lambda *refs: ffn_kernel(len(sizes), *refs), name='ffn', g...  30.4 us
    unnamed x38, local copies, waits for them, and re-layouts  8.27 us
  transfers between devices with their start and end apart: 49, of which 24 were waited for; matrix products, arithmetic and copies ran while one was open for 1% of the time, Pallas kernels for 13%

profile of v1, /device:TPU:0, one launch (start us, length us, event | category | flops | bytes accessed | tf_op | source)
XLA Modules:
  0.0 241.6 jit_solution(1891316396653178575)
XLA Ops:
  1.7 1.3 fusion.3
  5.2 1.7 collective-permute-start
  6.9 1.6 collective-permute-start.1
  8.9 2.9 %collective-permute-start.5 = (bf16[32,6144]{1,0:T(8,128)(2,1)S(1)}, bf16[32,6144]{1,0:T(8,128)(2,1)S(1)}, u32[]{:S(2)}, u32[]{:S(2)}) collective-permute-start(bf16[32,6144]{1,0:T(8,128)(2,1)S(1)} %get-tuple-element.65), channel_id=1, source_target_pairs={{0,96},{1,25},{2,98},{3,27},{4,100},{5,29},{6,102},{7,31},{8,104},... | collective-permute-start | bytes 1179656 | tf_op jit(solution)/shard_map/ppermute | solution.py:24
  11.8 2.5 %collective-permute-done = bf16[32,6144]{1,0:T(8,128)(2,1)S(1)} collective-permute-done((bf16[32,6144]{1,0:T(8,128)(2,1)S(1)}, bf16[32,6144]{1,0:T(8,128)(2,1)S(1)}, u32[]{:S(2)}, u32[]{:S(2)}) %collective-permute-start) | collective-permute-done | bytes 393248 | tf_op jit(solution)/shard_map/ppermute | solution.py:24
  14.8 2.9 %collective-permute-start.3 = (bf16[16,6144]{1,0:T(8,128)(2,1)S(1)}, bf16[16,6144]{1,0:T(8,128)(2,1)S(1)}, u32[]{:S(2)}, u32[]{:S(2)}) collective-permute-start(bf16[16,6144]{1,0:T(8,128)(2,1)S(1)} %slice.62), channel_id=1, source_target_pairs={{0,96},{1,25},{2,98},{3,27},{4,100},{5,29},{6,102},{7,31},{8,104},... | collective-permute-start | bytes 589832 | tf_op jit(solution)/shard_map/ppermute | solution.py:24
  19.0 2.9 %collective-permute-start.7 = (bf16[16,6144]{1,0:T(8,128)(2,1)S(1)}, bf16[16,6144]{1,0:T(8,128)(2,1)S(1)}, u32[]{:S(2)}, u32[]{:S(2)}) collective-permute-start(bf16[16,6144]{1,0:T(8,128)(2,1)S(1)} %slice.65), channel_id=1, source_target_pairs={{0,96},{1,25},{2,98},{3,27},{4,100},{5,29},{6,102},{7,31},{8,104},... | collective-permute-start | bytes 589832 | tf_op jit(solution)/shard_map/ppermute | solution.py:24
  22.1 3.4 %collective-permute-done.6 = bf16[16,6144]{1,0:T(8,128)(2,1)S(1)} collective-permute-done((bf16[16,6144]{1,0:T(8,128)(2,1)S(1)}, bf16[16,6144]{1,0:T(8,128)(2,1)S(1)}, u32[]{:S(2)}, u32[]{:S(2)}) %collective-permute-start.6) | collective-permute-done | bytes 196640 | tf_op jit(solution)/shard_map/ppermute | solution.py:24
  25.5 1.8 collective-permute-start.10
  27.3 1.6 collective-permute-start.12
  29.4 2.8 %collective-permute-start.19 = (bf16[128,6144]{1,0:T(8,128)(2,1)S(1)}, bf16[128,6144]{1,0:T(8,128)(2,1)S(1)}, u32[]{:S(2)}, u32[]{:S(2)}) collective-permute-start(bf16[128,6144]{1,0:T(8,128)(2,1)S(1)} %constant_dynamic-update-slice_fusion.refs_0_), channel_id=1, source_target_pairs={{0,24},{1,97},{2,26},{3,99},{4,28},{5,101},{6,30},{7,103},{8,0},{9... | collective-permute-start | bytes 4718600 | tf_op jit(solution)/shard_map/ppermute | solution.py:24
  32.2 15.0 %collective-permute-done.10 = bf16[128,6144]{1,0:T(8,128)(2,1)S(1)} collective-permute-done((bf16[128,6144]{1,0:T(8,128)(2,1)S(1)}, bf16[128,6144]{1,0:T(8,128)(2,1)S(1)}, u32[]{:S(2)}, u32[]{:S(2)}) %collective-permute-start.10) | collective-permute-done | bytes 1572896 | tf_op jit(solution)/shard_map/ppermute | solution.py:24
  47.9 2.8 %collective-permute-start.23 = (bf16[64,6144]{1,0:T(8,128)(2,1)S(1)}, bf16[64,6144]{1,0:T(8,128)(2,1)S(1)}, u32[]{:S(2)}, u32[]{:S(2)}) collective-permute-start(bf16[64,6144]{1,0:T(8,128)(2,1)S(1)} %slice.69), channel_id=1, source_target_pairs={{0,24},{1,97},{2,26},{3,99},{4,28},{5,101},{6,30},{7,103},{8,0},{9... | collective-permute-start | bytes 2359304 | tf_op jit(solution)/shard_map/ppermute | solution.py:24
  50.7 13.4 %collective-permute-done.17.refs_0_ = bf16[128,6144]{1,0:T(8,128)(2,1)S(1)} collective-permute-done((bf16[128,6144]{1,0:T(8,128)(2,1)S(1)}, bf16[128,6144]{1,0:T(8,128)(2,1)S(1)}, u32[]{:S(2)}, u32[]{:S(2)}) %collective-permute-start.17) | collective-permute-done | bytes 1572896 | tf_op jit(solution)/shard_map/ppermute | solution.py:24
  64.7 2.8 %collective-permute-start.20 = (bf16[64,6144]{1,0:T(8,128)(2,1)S(1)}, bf16[64,6144]{1,0:T(8,128)(2,1)S(1)}, u32[]{:S(2)}, u32[]{:S(2)}) collective-permute-start(bf16[64,6144]{1,0:T(8,128)(2,1)S(1)} %slice.67), channel_id=1, source_target_pairs={{0,24},{1,97},{2,26},{3,99},{4,28},{5,101},{6,30},{7,103},{8,0},{9... | collective-permute-start | bytes 2359304 | tf_op jit(solution)/shard_map/ppermute | solution.py:24
  67.5 4.9 %collective-permute-done.21 = bf16[64,6144]{1,0:T(8,128)(2,1)S(1)} collective-permute-done((bf16[64,6144]{1,0:T(8,128)(2,1)S(1)}, bf16[64,6144]{1,0:T(8,128)(2,1)S(1)}, u32[]{:S(2)}, u32[]{:S(2)}) %collective-permute-start.21) | collective-permute-done | bytes 786464 | tf_op jit(solution)/shard_map/ppermute | solution.py:24
  73.5 7.4 %collective-permute-done.18.refs_0_ = bf16[64,6144]{1,0:T(8,128)(2,1)S(1)} collective-permute-done((bf16[64,6144]{1,0:T(8,128)(2,1)S(1)}, bf16[64,6144]{1,0:T(8,128)(2,1)S(1)}, u32[]{:S(2)}, u32[]{:S(2)}) %collective-permute-start.18) | collective-permute-done | bytes 786464 | tf_op jit(solution)/shard_map/ppermute | solution.py:24
  80.9 2.8 %copy-done.3 = bf16[1,512,6144]{2,1,0:T(8,128)(2,1)S(1)} copy-done((bf16[1,512,6144]{2,1,0:T(8,128)(2,1)S(1)}, bf16[1,512,6144]{2,1,0:T(8,128)(2,1)}, u32[]{:S(2)}) %copy-start.3) | copy-done | bytes 6291480
  83.7 7.6 %ffn.4 = (bf16[64,6144]{1,0:T(8,128)(2,1)S(1)}, bf16[64,6144]{1,0:T(8,128)(2,1)S(1)}, bf16[64,6144]{1,0:T(8,128)(2,1)S(1)}, bf16[64,6144]{1,0:T(8,128)(2,1)S(1)}) custom-call(bf16[128,6144]{1,0:T(8,128)(2,1)S(1)} %constant_dynamic-update-slice_fusion.refs_0_, bf16[128,6144]{1,0:T(8,128)(2,1)S(1)} %collective-permute-done.8.refs_1_, ...), custom_call_target="tpu_custom_call" | custom-call | flops 4831838208 | bytes 25165824 | tf_op jit(solution)/shard_map/ffn/pallas_call | solution.py:192
  92.2 7.7 %ffn.6 = (bf16[64,6144]{1,0:T(8,128)(2,1)S(1)}, bf16[64,6144]{1,0:T(8,128)(2,1)S(1)}, bf16[64,6144]{1,0:T(8,128)(2,1)S(1)}, bf16[64,6144]{1,0:T(8,128)(2,1)S(1)}) custom-call(bf16[64,6144]{1,0:T(8,128)(2,1)S(1)} %collective-permute-done.18.refs_0_, bf16[64,6144]{1,0:T(8,128)(2,1)S(1)} %collective-permute-done.20.refs_1_, ...), custom_call_target="tpu_custom_call" | custom-call | flops 4831838208 | bytes 25165824 | tf_op jit(solution)/shard_map/ffn/pallas_call | solution.py:192
  99.9 2.0 collective-permute-start.36
  101.9 7.6 %ffn.7 = (bf16[64,6144]{1,0:T(8,128)(2,1)S(1)}, bf16[64,6144]{1,0:T(8,128)(2,1)S(1)}, bf16[64,6144]{1,0:T(8,128)(2,1)S(1)}, bf16[64,6144]{1,0:T(8,128)(2,1)S(1)}) custom-call(bf16[128,6144]{1,0:T(8,128)(2,1)S(1)} %collective-permute-done.17.refs_0_, bf16[128,6144]{1,0:T(8,128)(2,1)S(1)} %collective-permute-done.19.refs_1_, ...), custom_call_target="tpu_custom_call" | custom-call | flops 4831838208 | bytes 25165824 | tf_op jit(solution)/shard_map/ffn/pallas_call | solution.py:192
  109.5 1.4 collective-permute-start.25
  110.9 7.6 %ffn.5 = (bf16[64,6144]{1,0:T(8,128)(2,1)S(1)}, bf16[64,6144]{1,0:T(8,128)(2,1)S(1)}, bf16[64,6144]{1,0:T(8,128)(2,1)S(1)}, bf16[64,6144]{1,0:T(8,128)(2,1)S(1)}) custom-call(bf16[128,6144]{1,0:T(8,128)(2,1)S(1)} %collective-permute-done.11.refs_0_, bf16[128,6144]{1,0:T(8,128)(2,1)S(1)} %collective-permute-done.13.refs_1_, ...), custom_call_target="tpu_custom_call" | custom-call | flops 4831838208 | bytes 25165824 | tf_op jit(solution)/shard_map/ffn/pallas_call | solution.py:192
  119.4 12.4 %collective-permute-done.39 = bf16[64,6144]{1,0:T(8,128)(2,1)S(1)} collective-permute-done((bf16[64,6144]{1,0:T(8,128)(2,1)S(1)}, bf16[64,6144]{1,0:T(8,128)(2,1)S(1)}, u32[]{:S(2)}, u32[]{:S(2)}) %collective-permute-start.39) | collective-permute-done | bytes 786464 | tf_op jit(solution)/shard_map/ppermute | solution.py:24
  133.4 10.5 %collective-permute-done.26 = bf16[64,6144]{1,0:T(8,128)(2,1)S(1)} collective-permute-done((bf16[64,6144]{1,0:T(8,128)(2,1)S(1)}, bf16[64,6144]{1,0:T(8,128)(2,1)S(1)}, u32[]{:S(2)}, u32[]{:S(2)}) %collective-permute-start.26) | collective-permute-done | bytes 786464 | tf_op jit(solution)/shard_map/ppermute | solution.py:24
  145.0 2.5 %collective-permute-start.38 = (bf16[64,6144]{1,0:T(8,128)(2,1)S(1)}, bf16[64,6144]{1,0:T(8,128)(2,1)S(1)}, u32[]{:S(2)}, u32[]{:S(2)}) collective-permute-start(bf16[64,6144]{1,0:T(8,128)(2,1)S(1)} %get-tuple-element.45), channel_id=1, source_target_pairs={{0,24},{1,97},{2,26},{3,99},{4,28},{5,101},{6,30},{7,103},{8,0},{9... | collective-permute-start | bytes 2359304 | tf_op jit(solution)/shard_map/ppermute | solution.py:24
  147.5 9.6 %collective-permute-done.33 = bf16[64,6144]{1,0:T(8,128)(2,1)S(1)} collective-permute-done((bf16[64,6144]{1,0:T(8,128)(2,1)S(1)}, bf16[64,6144]{1,0:T(8,128)(2,1)S(1)}, u32[]{:S(2)}, u32[]{:S(2)}) %collective-permute-start.33) | collective-permute-done | bytes 786464 | tf_op jit(solution)/shard_map/ppermute | solution.py:24
  157.3 3.3 %collective-permute-start.37 = (bf16[64,6144]{1,0:T(8,128)(2,1)S(1)}, bf16[64,6144]{1,0:T(8,128)(2,1)S(1)}, u32[]{:S(2)}, u32[]{:S(2)}) collective-permute-start(bf16[64,6144]{1,0:T(8,128)(2,1)S(1)} %add_convert_fusion.1), channel_id=1, source_target_pairs={{0,24},{1,97},{2,26},{3,99},{4,28},{5,101},{6,30},{7,103},{8,0},{9... | collective-permute-start | bytes 2359304 | tf_op jit(solution)/shard_map/ppermute | solution.py:24
  160.6 4.9 %collective-permute-done.35.refs_7_ = bf16[64,6144]{1,0:T(8,128)(2,1)S(1)} collective-permute-done((bf16[64,6144]{1,0:T(8,128)(2,1)S(1)}, bf16[64,6144]{1,0:T(8,128)(2,1)S(1)}, u32[]{:S(2)}, u32[]{:S(2)}) %collective-permute-start.35) | collective-permute-done | bytes 786464 | tf_op jit(solution)/shard_map/ppermute | solution.py:24
  165.5 3.2 %collective-permute-start.30 = (bf16[64,6144]{1,0:T(8,128)(2,1)S(1)}, bf16[64,6144]{1,0:T(8,128)(2,1)S(1)}, u32[]{:S(2)}, u32[]{:S(2)}) collective-permute-start(bf16[64,6144]{1,0:T(8,128)(2,1)S(1)} %collective-permute-done.29), channel_id=1, source_target_pairs={{0,24},{1,97},{2,26},{3,99},{4,28},{5,101},{6,30},{7,103},{8,0},{9... | collective-permute-start | bytes 2359304 | tf_op jit(solution)/shard_map/ppermute | solution.py:24
  168.8 5.1 %collective-permute-done.15.refs_1_ = bf16[64,6144]{1,0:T(8,128)(2,1)S(1)} collective-permute-done((bf16[64,6144]{1,0:T(8,128)(2,1)S(1)}, bf16[64,6144]{1,0:T(8,128)(2,1)S(1)}, u32[]{:S(2)}, u32[]{:S(2)}) %collective-permute-start.15) | collective-permute-done | bytes 786464 | tf_op jit(solution)/shard_map/ppermute | solution.py:24
  173.9 4.6 %collective-permute-done.30.refs_4_ = bf16[64,6144]{1,0:T(8,128)(2,1)S(1)} collective-permute-done((bf16[64,6144]{1,0:T(8,128)(2,1)S(1)}, bf16[64,6144]{1,0:T(8,128)(2,1)S(1)}, u32[]{:S(2)}, u32[]{:S(2)}) %collective-permute-start.30) | collective-permute-done | bytes 786464 | tf_op jit(solution)/shard_map/ppermute | solution.py:24
  178.5 3.8 %collective-permute-done.40.refs_11_ = bf16[64,6144]{1,0:T(8,128)(2,1)S(1)} collective-permute-done((bf16[64,6144]{1,0:T(8,128)(2,1)S(1)}, bf16[64,6144]{1,0:T(8,128)(2,1)S(1)}, u32[]{:S(2)}, u32[]{:S(2)}) %collective-permute-start.40) | collective-permute-done | bytes 786464 | tf_op jit(solution)/shard_map/ppermute | solution.py:24
  182.3 4.6 %collective-permute-done.27.refs_2_ = bf16[64,6144]{1,0:T(8,128)(2,1)S(1)} collective-permute-done((bf16[64,6144]{1,0:T(8,128)(2,1)S(1)}, bf16[64,6144]{1,0:T(8,128)(2,1)S(1)}, u32[]{:S(2)}, u32[]{:S(2)}) %collective-permute-start.27) | collective-permute-done | bytes 786464 | tf_op jit(solution)/shard_map/ppermute | solution.py:24
  186.9 3.8 %collective-permute-done.34.refs_5_ = bf16[64,6144]{1,0:T(8,128)(2,1)S(1)} collective-permute-done((bf16[64,6144]{1,0:T(8,128)(2,1)S(1)}, bf16[64,6144]{1,0:T(8,128)(2,1)S(1)}, u32[]{:S(2)}, u32[]{:S(2)}) %collective-permute-start.34) | collective-permute-done | bytes 786464 | tf_op jit(solution)/shard_map/ppermute | solution.py:24
  190.8 1.2 shard_map.73
  192.0 2.4 %collective-permute-start.41 = (bf16[64,6144]{1,0:T(8,128)(2,1)S(1)}, bf16[64,6144]{1,0:T(8,128)(2,1)S(1)}, u32[]{:S(2)}, u32[]{:S(2)}) collective-permute-start(bf16[64,6144]{1,0:T(8,128)(2,1)S(1)} %get-tuple-element.49), channel_id=1, source_target_pairs={{0,96},{1,25},{2,98},{3,27},{4,100},{5,29},{6,102},{7,31},{8,104},... | collective-permute-start | bytes 2359304 | tf_op jit(solution)/shard_map/ppermute | solution.py:24
  194.4 9.6 %collective-permute-done.41.from_minus = bf16[64,6144]{1,0:T(8,128)(2,1)S(1)} collective-permute-done((bf16[64,6144]{1,0:T(8,128)(2,1)S(1)}, bf16[64,6144]{1,0:T(8,128)(2,1)S(1)}, u32[]{:S(2)}, u32[]{:S(2)}) %collective-permute-start.41) | collective-permute-done | bytes 786464 | tf_op jit(solution)/shard_map/ppermute | solution.py:24
  204.1 3.9 %collective-permute-start.43 = (bf16[32,6144]{1,0:T(8,128)(2,1)S(1)}, bf16[32,6144]{1,0:T(8,128)(2,1)S(1)}, u32[]{:S(2)}, u32[]{:S(2)}) collective-permute-start(bf16[32,6144]{1,0:T(8,128)(2,1)S(1)} %add_convert_fusion.5), channel_id=1, source_target_pairs={{0,96},{1,25},{2,98},{3,27},{4,100},{5,29},{6,102},{7,31},{8,104},... | collective-permute-start | bytes 1179656 | tf_op jit(solution)/shard_map/ppermute | solution.py:24
  208.3 5.0 %collective-permute-done.43.near_after = bf16[32,6144]{1,0:T(8,128)(2,1)S(1)} collective-permute-done((bf16[32,6144]{1,0:T(8,128)(2,1)S(1)}, bf16[32,6144]{1,0:T(8,128)(2,1)S(1)}, u32[]{:S(2)}, u32[]{:S(2)}) %collective-permute-start.43) | collective-permute-done | bytes 393248 | tf_op jit(solution)/shard_map/ppermute | solution.py:24
  213.3 3.8 %collective-permute-done.44.near_before = bf16[32,6144]{1,0:T(8,128)(2,1)S(1)} collective-permute-done((bf16[32,6144]{1,0:T(8,128)(2,1)S(1)}, bf16[32,6144]{1,0:T(8,128)(2,1)S(1)}, u32[]{:S(2)}, u32[]{:S(2)}) %collective-permute-start.44) | collective-permute-done | bytes 393248 | tf_op jit(solution)/shard_map/ppermute | solution.py:24
  217.9 1.4 copy-done.5
  220.3 1.6 shard_map.74
  226.7 4.0 %collective-permute-start.46 = (bf16[128,768]{1,0:T(8,128)(2,1)S(1)}, bf16[128,768]{1,0:T(8,128)(2,1)S(1)}, u32[]{:S(2)}, u32[]{:S(2)}) collective-permute-start(bf16[128,768]{1,0:T(8,128)(2,1)S(1)} %get-tuple-element.56), channel_id=1, source_target_pairs={{0,4},{1,5},{2,6},{3,7},{4,0},{5,1},{6,2},{7,3},{8,12},{9,13},{10,... | collective-permute-start | bytes 589832 | tf_op jit(solution)/shard_map/ppermute | solution.py:24
  231.7 2.2 collective-permute-start.48
  233.9 2.5 %collective-permute-done.46.refs_0_ = bf16[128,768]{1,0:T(8,128)(2,1)S(1)} collective-permute-done((bf16[128,768]{1,0:T(8,128)(2,1)S(1)}, bf16[128,768]{1,0:T(8,128)(2,1)S(1)}, u32[]{:S(2)}, u32[]{:S(2)}) %collective-permute-start.46) | collective-permute-done | bytes 196640 | tf_op jit(solution)/shard_map/ppermute | solution.py:24
  236.4 3.7 %collective-permute-done.47.refs_1_ = bf16[128,768]{1,0:T(8,128)(2,1)S(1)} collective-permute-done((bf16[128,768]{1,0:T(8,128)(2,1)S(1)}, bf16[128,768]{1,0:T(8,128)(2,1)S(1)}, u32[]{:S(2)}, u32[]{:S(2)}) %collective-permute-start.47) | collective-permute-done | bytes 196640 | tf_op jit(solution)/shard_map/ppermute | solution.py:24
  (135 shorter events, 23.0 us)
Async XLA Ops:
  5.2 9.1 %collective-permute-start = (bf16[32,6144]{1,0:T(8,128)(2,1)S(1)}, bf16[32,6144]{1,0:T(8,128)(2,1)S(1)}, u32[]{:S(2)}, u32[]{:S(2)}) collective-permute-start(bf16[32,6144]{1,0:T(8,128)(2,1)S(1)} %get-tuple-element.68), channel_id=1, source_target_pairs={{0,32},{1,9},{2,34},{3,11},{4,36},{5,13},{6,38},{7,15},{8,40},{9,1... | collective-permute-start | bytes 1179656 | tf_op jit(solution)/shard_map/ppermute | solution.py:24
  6.9 7.9 %collective-permute-start.1 = (bf16[32,6144]{1,0:T(8,128)(2,1)S(1)}, bf16[32,6144]{1,0:T(8,128)(2,1)S(1)}, u32[]{:S(2)}, u32[]{:S(2)}) collective-permute-start(bf16[32,6144]{1,0:T(8,128)(2,1)S(1)} %get-tuple-element.68), channel_id=1, source_target_pairs={{0,96},{1,25},{2,98},{3,27},{4,100},{5,29},{6,102},{7,31},{8,104},... | collective-permute-start | bytes 1179656 | tf_op jit(solution)/shard_map/ppermute | solution.py:24
  8.5 10.0 %collective-permute-start.4 = (bf16[32,6144]{1,0:T(8,128)(2,1)S(1)}, bf16[32,6144]{1,0:T(8,128)(2,1)S(1)}, u32[]{:S(2)}, u32[]{:S(2)}) collective-permute-start(bf16[32,6144]{1,0:T(8,128)(2,1)S(1)} %get-tuple-element.65), channel_id=1, source_target_pairs={{0,32},{1,9},{2,34},{3,11},{4,36},{5,13},{6,38},{7,15},{8,40},{9,1... | collective-permute-start | bytes 1179656 | tf_op jit(solution)/shard_map/ppermute | solution.py:24
  8.9 10.1 %collective-permute-start.5 = (bf16[32,6144]{1,0:T(8,128)(2,1)S(1)}, bf16[32,6144]{1,0:T(8,128)(2,1)S(1)}, u32[]{:S(2)}, u32[]{:S(2)}) collective-permute-start(bf16[32,6144]{1,0:T(8,128)(2,1)S(1)} %get-tuple-element.65), channel_id=1, source_target_pairs={{0,96},{1,25},{2,98},{3,27},{4,100},{5,29},{6,102},{7,31},{8,104},... | collective-permute-start | bytes 1179656 | tf_op jit(solution)/shard_map/ppermute | solution.py:24
  14.3 14.5 %collective-permute-start.2 = (bf16[16,6144]{1,0:T(8,128)(2,1)S(1)}, bf16[16,6144]{1,0:T(8,128)(2,1)S(1)}, u32[]{:S(2)}, u32[]{:S(2)}) collective-permute-start(bf16[16,6144]{1,0:T(8,128)(2,1)S(1)} %slice.61), channel_id=1, source_target_pairs={{0,32},{1,9},{2,34},{3,11},{4,36},{5,13},{6,38},{7,15},{8,40},{9,1... | collective-permute-start | bytes 589832 | tf_op jit(solution)/shard_map/ppermute | solution.py:24
  14.8 14.1 %collective-permute-start.3 = (bf16[16,6144]{1,0:T(8,128)(2,1)S(1)}, bf16[16,6144]{1,0:T(8,128)(2,1)S(1)}, u32[]{:S(2)}, u32[]{:S(2)}) collective-permute-start(bf16[16,6144]{1,0:T(8,128)(2,1)S(1)} %slice.62), channel_id=1, source_target_pairs={{0,96},{1,25},{2,98},{3,27},{4,100},{5,29},{6,102},{7,31},{8,104},... | collective-permute-start | bytes 589832 | tf_op jit(solution)/shard_map/ppermute | solution.py:24
  18.5 6.9 %collective-permute-start.6 = (bf16[16,6144]{1,0:T(8,128)(2,1)S(1)}, bf16[16,6144]{1,0:T(8,128)(2,1)S(1)}, u32[]{:S(2)}, u32[]{:S(2)}) collective-permute-start(bf16[16,6144]{1,0:T(8,128)(2,1)S(1)} %slice.64), channel_id=1, source_target_pairs={{0,32},{1,9},{2,34},{3,11},{4,36},{5,13},{6,38},{7,15},{8,40},{9,1... | collective-permute-start | bytes 589832 | tf_op jit(solution)/shard_map/ppermute | solution.py:24
  19.0 6.5 %collective-permute-start.7 = (bf16[16,6144]{1,0:T(8,128)(2,1)S(1)}, bf16[16,6144]{1,0:T(8,128)(2,1)S(1)}, u32[]{:S(2)}, u32[]{:S(2)}) collective-permute-start(bf16[16,6144]{1,0:T(8,128)(2,1)S(1)} %slice.65), channel_id=1, source_target_pairs={{0,96},{1,25},{2,98},{3,27},{4,100},{5,29},{6,102},{7,31},{8,104},... | collective-permute-start | bytes 589832 | tf_op jit(solution)/shard_map/ppermute | solution.py:24
  25.5 21.7 %collective-permute-start.10 = (bf16[128,6144]{1,0:T(8,128)(2,1)S(1)}, bf16[128,6144]{1,0:T(8,128)(2,1)S(1)}, u32[]{:S(2)}, u32[]{:S(2)}) collective-permute-start(bf16[128,6144]{1,0:T(8,128)(2,1)S(1)} %constant_dynamic-update-slice_fusion.5), channel_id=1, source_target_pairs={{0,8},{1,33},{2,10},{3,35},{4,12},{5,37},{6,14},{7,39},{8,16},{9,4... | collective-permute-start | bytes 4718600 | tf_op jit(solution)/shard_map/ppermute | solution.py:24
  27.3 20.5 %collective-permute-start.12 = (bf16[128,6144]{1,0:T(8,128)(2,1)S(1)}, bf16[128,6144]{1,0:T(8,128)(2,1)S(1)}, u32[]{:S(2)}, u32[]{:S(2)}) collective-permute-start(bf16[128,6144]{1,0:T(8,128)(2,1)S(1)} %constant_dynamic-update-slice_fusion.5), channel_id=1, source_target_pairs={{0,24},{1,97},{2,26},{3,99},{4,28},{5,101},{6,30},{7,103},{8,0},{9... | collective-permute-start | bytes 4718600 | tf_op jit(solution)/shard_map/ppermute | solution.py:24
  28.9 35.2 %collective-permute-start.17 = (bf16[128,6144]{1,0:T(8,128)(2,1)S(1)}, bf16[128,6144]{1,0:T(8,128)(2,1)S(1)}, u32[]{:S(2)}, u32[]{:S(2)}) collective-permute-start(bf16[128,6144]{1,0:T(8,128)(2,1)S(1)} %constant_dynamic-update-slice_fusion.refs_0_), channel_id=1, source_target_pairs={{0,8},{1,33},{2,10},{3,35},{4,12},{5,37},{6,14},{7,39},{8,16},{9,4... | collective-permute-start | bytes 4718600 | tf_op jit(solution)/shard_map/ppermute | solution.py:24
  29.4 35.2 %collective-permute-start.19 = (bf16[128,6144]{1,0:T(8,128)(2,1)S(1)}, bf16[128,6144]{1,0:T(8,128)(2,1)S(1)}, u32[]{:S(2)}, u32[]{:S(2)}) collective-permute-start(bf16[128,6144]{1,0:T(8,128)(2,1)S(1)} %constant_dynamic-update-slice_fusion.refs_0_), channel_id=1, source_target_pairs={{0,24},{1,97},{2,26},{3,99},{4,28},{5,101},{6,30},{7,103},{8,0},{9... | collective-permute-start | bytes 4718600 | tf_op jit(solution)/shard_map/ppermute | solution.py:24
  32.2 40.8 %collective-permute-start.8 = (bf16[128,6144]{1,0:T(8,128)(2,1)S(1)}, bf16[128,6144]{1,0:T(8,128)(2,1)S(1)}, u32[]{:S(2)}, u32[]{:S(2)}) collective-permute-start(bf16[128,6144]{1,0:T(8,128)(2,1)S(1)} %constant_dynamic-update-slice_fusion.5), channel_id=1, source_target_pairs={{0,1},{1,0},{2,3},{3,2},{4,5},{5,4},{6,7},{7,6},{8,9},{9,8},{10,11... | collective-permute-start | bytes 4718600 | tf_op jit(solution)/shard_map/ppermute | solution.py:24
  47.3 25.2 %collective-permute-start.21 = (bf16[64,6144]{1,0:T(8,128)(2,1)S(1)}, bf16[64,6144]{1,0:T(8,128)(2,1)S(1)}, u32[]{:S(2)}, u32[]{:S(2)}) collective-permute-start(bf16[64,6144]{1,0:T(8,128)(2,1)S(1)} %slice.68), channel_id=1, source_target_pairs={{0,8},{1,33},{2,10},{3,35},{4,12},{5,37},{6,14},{7,39},{8,16},{9,4... | collective-permute-start | bytes 2359304 | tf_op jit(solution)/shard_map/ppermute | solution.py:24
  47.9 25.1 %collective-permute-start.23 = (bf16[64,6144]{1,0:T(8,128)(2,1)S(1)}, bf16[64,6144]{1,0:T(8,128)(2,1)S(1)}, u32[]{:S(2)}, u32[]{:S(2)}) collective-permute-start(bf16[64,6144]{1,0:T(8,128)(2,1)S(1)} %slice.69), channel_id=1, source_target_pairs={{0,24},{1,97},{2,26},{3,99},{4,28},{5,101},{6,30},{7,103},{8,0},{9... | collective-permute-start | bytes 2359304 | tf_op jit(solution)/shard_map/ppermute | solution.py:24
  64.1 16.8 %collective-permute-start.18 = (bf16[64,6144]{1,0:T(8,128)(2,1)S(1)}, bf16[64,6144]{1,0:T(8,128)(2,1)S(1)}, u32[]{:S(2)}, u32[]{:S(2)}) collective-permute-start(bf16[64,6144]{1,0:T(8,128)(2,1)S(1)} %slice.66), channel_id=1, source_target_pairs={{0,8},{1,33},{2,10},{3,35},{4,12},{5,37},{6,14},{7,39},{8,16},{9,4... | collective-permute-start | bytes 2359304 | tf_op jit(solution)/shard_map/ppermute | solution.py:24
  64.7 26.6 %collective-permute-start.20 = (bf16[64,6144]{1,0:T(8,128)(2,1)S(1)}, bf16[64,6144]{1,0:T(8,128)(2,1)S(1)}, u32[]{:S(2)}, u32[]{:S(2)}) collective-permute-start(bf16[64,6144]{1,0:T(8,128)(2,1)S(1)} %slice.67), channel_id=1, source_target_pairs={{0,24},{1,97},{2,26},{3,99},{4,28},{5,101},{6,30},{7,103},{8,0},{9... | collective-permute-start | bytes 2359304 | tf_op jit(solution)/shard_map/ppermute | solution.py:24
  72.5 19.4 %collective-permute-start.22 = (bf16[64,6144]{1,0:T(8,128)(2,1)S(1)}, bf16[64,6144]{1,0:T(8,128)(2,1)S(1)}, u32[]{:S(2)}, u32[]{:S(2)}) collective-permute-start(bf16[64,6144]{1,0:T(8,128)(2,1)S(1)} %collective-permute-done.21), channel_id=1, source_target_pairs={{0,1},{1,0},{2,3},{3,2},{4,5},{5,4},{6,7},{7,6},{8,9},{9,8},{10,11... | collective-permute-start | bytes 2359304 | tf_op jit(solution)/shard_map/ppermute | solution.py:24
  73.0 19.2 %collective-permute-start.24 = (bf16[64,6144]{1,0:T(8,128)(2,1)S(1)}, bf16[64,6144]{1,0:T(8,128)(2,1)S(1)}, u32[]{:S(2)}, u32[]{:S(2)}) collective-permute-start(bf16[64,6144]{1,0:T(8,128)(2,1)S(1)} %collective-permute-done.23), channel_id=1, source_target_pairs={{0,1},{1,0},{2,3},{3,2},{4,5},{5,4},{6,7},{7,6},{8,9},{9,8},{10,11... | collective-permute-start | bytes 2359304 | tf_op jit(solution)/shard_map/ppermute | solution.py:24
  73.0 36.5 %collective-permute-start.11 = (bf16[128,6144]{1,0:T(8,128)(2,1)S(1)}, bf16[128,6144]{1,0:T(8,128)(2,1)S(1)}, u32[]{:S(2)}, u32[]{:S(2)}) collective-permute-start(bf16[128,6144]{1,0:T(8,128)(2,1)S(1)} %collective-permute-done.10), channel_id=1, source_target_pairs={{0,1},{1,0},{2,3},{3,2},{4,5},{5,4},{6,7},{7,6},{8,9},{9,8},{10,11... | collective-permute-start | bytes 4718600 | tf_op jit(solution)/shard_map/ppermute | solution.py:24
  80.9 30.0 %collective-permute-start.13 = (bf16[128,6144]{1,0:T(8,128)(2,1)S(1)}, bf16[128,6144]{1,0:T(8,128)(2,1)S(1)}, u32[]{:S(2)}, u32[]{:S(2)}) collective-permute-start(bf16[128,6144]{1,0:T(8,128)(2,1)S(1)} %collective-permute-done.12), channel_id=1, source_target_pairs={{0,1},{1,0},{2,3},{3,2},{4,5},{5,4},{6,7},{7,6},{8,9},{9,8},{10,11... | collective-permute-start | bytes 4718600 | tf_op jit(solution)/shard_map/ppermute | solution.py:24
  91.3 52.7 %collective-permute-start.9 = (bf16[64,6144]{1,0:T(8,128)(2,1)S(1)}, bf16[64,6144]{1,0:T(8,128)(2,1)S(1)}, u32[]{:S(2)}, u32[]{:S(2)}) collective-permute-start(bf16[64,6144]{1,0:T(8,128)(2,1)S(1)} %get-tuple-element.32), channel_id=1, source_target_pairs={{0,1},{1,0},{2,3},{3,2},{4,5},{5,4},{6,7},{7,6},{8,9},{9,8},{10,11... | collective-permute-start | bytes 2359304 | tf_op jit(solution)/shard_map/ppermute | solution.py:24
  91.9 65.3 %collective-permute-start.28 = (bf16[64,6144]{1,0:T(8,128)(2,1)S(1)}, bf16[64,6144]{1,0:T(8,128)(2,1)S(1)}, u32[]{:S(2)}, u32[]{:S(2)}) collective-permute-start(bf16[64,6144]{1,0:T(8,128)(2,1)S(1)} %get-tuple-element.36), channel_id=1, source_target_pairs={{0,1},{1,0},{2,3},{3,2},{4,5},{5,4},{6,7},{7,6},{8,9},{9,8},{10,11... | collective-permute-start | bytes 2359304 | tf_op jit(solution)/shard_map/ppermute | solution.py:24
  99.9 18.7 %collective-permute-start.36 = (bf16[64,6144]{1,0:T(8,128)(2,1)S(1)}, bf16[64,6144]{1,0:T(8,128)(2,1)S(1)}, u32[]{:S(2)}, u32[]{:S(2)}) collective-permute-start(bf16[64,6144]{1,0:T(8,128)(2,1)S(1)} %get-tuple-element.43), channel_id=1, source_target_pairs={{0,24},{1,97},{2,26},{3,99},{4,28},{5,101},{6,30},{7,103},{8,0},{9... | collective-permute-start | bytes 2359304 | tf_op jit(solution)/shard_map/ppermute | solution.py:24
  109.5 9.9 %collective-permute-start.25 = (bf16[64,6144]{1,0:T(8,128)(2,1)S(1)}, bf16[64,6144]{1,0:T(8,128)(2,1)S(1)}, u32[]{:S(2)}, u32[]{:S(2)}) collective-permute-start(bf16[64,6144]{1,0:T(8,128)(2,1)S(1)} %get-tuple-element.35), channel_id=1, source_target_pairs={{0,1},{1,0},{2,3},{3,2},{4,5},{5,4},{6,7},{7,6},{8,9},{9,8},{10,11... | collective-permute-start | bytes 2359304 | tf_op jit(solution)/shard_map/ppermute | solution.py:24
  118.5 14.3 %collective-permute-start.16 = (bf16[64,6144]{1,0:T(8,128)(2,1)S(1)}, bf16[64,6144]{1,0:T(8,128)(2,1)S(1)}, u32[]{:S(2)}, u32[]{:S(2)}) collective-permute-start(bf16[64,6144]{1,0:T(8,128)(2,1)S(1)} %get-tuple-element.34), channel_id=1, source_target_pairs={{0,1},{1,0},{2,3},{3,2},{4,5},{5,4},{6,7},{7,6},{8,9},{9,8},{10,11... | collective-permute-start | bytes 2359304 | tf_op jit(solution)/shard_map/ppermute | solution.py:24
  118.6 13.3 %collective-permute-start.39 = (bf16[64,6144]{1,0:T(8,128)(2,1)S(1)}, bf16[64,6144]{1,0:T(8,128)(2,1)S(1)}, u32[]{:S(2)}, u32[]{:S(2)}) collective-permute-start(bf16[64,6144]{1,0:T(8,128)(2,1)S(1)} %get-tuple-element.47), channel_id=1, source_target_pairs={{0,8},{1,33},{2,10},{3,35},{4,12},{5,37},{6,14},{7,39},{8,16},{9,4... | collective-permute-start | bytes 2359304 | tf_op jit(solution)/shard_map/ppermute | solution.py:24
  119.3 13.5 %collective-permute-start.32 = (bf16[64,6144]{1,0:T(8,128)(2,1)S(1)}, bf16[64,6144]{1,0:T(8,128)(2,1)S(1)}, u32[]{:S(2)}, u32[]{:S(2)}) collective-permute-start(bf16[64,6144]{1,0:T(8,128)(2,1)S(1)} %get-tuple-element.39), channel_id=1, source_target_pairs={{0,1},{1,0},{2,3},{3,2},{4,5},{5,4},{6,7},{7,6},{8,9},{9,8},{10,11... | collective-permute-start | bytes 2359304 | tf_op jit(solution)/shard_map/ppermute | solution.py:24
  131.9 12.0 %collective-permute-start.26 = (bf16[64,6144]{1,0:T(8,128)(2,1)S(1)}, bf16[64,6144]{1,0:T(8,128)(2,1)S(1)}, u32[]{:S(2)}, u32[]{:S(2)}) collective-permute-start(bf16[64,6144]{1,0:T(8,128)(2,1)S(1)} %collective-permute-done.25), channel_id=1, source_target_pairs={{0,24},{1,97},{2,26},{3,99},{4,28},{5,101},{6,30},{7,103},{8,0},{9... | collective-permute-start | bytes 2359304 | tf_op jit(solution)/shard_map/ppermute | solution.py:24
  132.8 12.2 %collective-permute-start.14 = (bf16[64,6144]{1,0:T(8,128)(2,1)S(1)}, bf16[64,6144]{1,0:T(8,128)(2,1)S(1)}, u32[]{:S(2)}, u32[]{:S(2)}) collective-permute-start(bf16[64,6144]{1,0:T(8,128)(2,1)S(1)} %get-tuple-element.33), channel_id=1, source_target_pairs={{0,1},{1,0},{2,3},{3,2},{4,5},{5,4},{6,7},{7,6},{8,9},{9,8},{10,11... | collective-permute-start | bytes 2359304 | tf_op jit(solution)/shard_map/ppermute | solution.py:24
  132.9 14.6 %collective-permute-start.31 = (bf16[64,6144]{1,0:T(8,128)(2,1)S(1)}, bf16[64,6144]{1,0:T(8,128)(2,1)S(1)}, u32[]{:S(2)}, u32[]{:S(2)}) collective-permute-start(bf16[64,6144]{1,0:T(8,128)(2,1)S(1)} %get-tuple-element.38), channel_id=1, source_target_pairs={{0,1},{1,0},{2,3},{3,2},{4,5},{5,4},{6,7},{7,6},{8,9},{9,8},{10,11... | collective-permute-start | bytes 2359304 | tf_op jit(solution)/shard_map/ppermute | solution.py:24
  143.9 13.2 %collective-permute-start.33 = (bf16[64,6144]{1,0:T(8,128)(2,1)S(1)}, bf16[64,6144]{1,0:T(8,128)(2,1)S(1)}, u32[]{:S(2)}, u32[]{:S(2)}) collective-permute-start(bf16[64,6144]{1,0:T(8,128)(2,1)S(1)} %collective-permute-done.32), channel_id=1, source_target_pairs={{0,8},{1,33},{2,10},{3,35},{4,12},{5,37},{6,14},{7,39},{8,16},{9,4... | collective-permute-start | bytes 2359304 | tf_op jit(solution)/shard_map/ppermute | solution.py:24
  144.1 21.4 %collective-permute-start.35 = (bf16[64,6144]{1,0:T(8,128)(2,1)S(1)}, bf16[64,6144]{1,0:T(8,128)(2,1)S(1)}, u32[]{:S(2)}, u32[]{:S(2)}) collective-permute-start(bf16[64,6144]{1,0:T(8,128)(2,1)S(1)} %get-tuple-element.41), channel_id=1, source_target_pairs={{0,8},{1,33},{2,10},{3,35},{4,12},{5,37},{6,14},{7,39},{8,16},{9,4... | collective-permute-start | bytes 2359304 | tf_op jit(solution)/shard_map/ppermute | solution.py:24
  145.0 23.8 %collective-permute-start.38 = (bf16[64,6144]{1,0:T(8,128)(2,1)S(1)}, bf16[64,6144]{1,0:T(8,128)(2,1)S(1)}, u32[]{:S(2)}, u32[]{:S(2)}) collective-permute-start(bf16[64,6144]{1,0:T(8,128)(2,1)S(1)} %get-tuple-element.45), channel_id=1, source_target_pairs={{0,24},{1,97},{2,26},{3,99},{4,28},{5,101},{6,30},{7,103},{8,0},{9... | collective-permute-start | bytes 2359304 | tf_op jit(solution)/shard_map/ppermute | solution.py:24
  147.5 18.0 %collective-permute-start.29 = (bf16[64,6144]{1,0:T(8,128)(2,1)S(1)}, bf16[64,6144]{1,0:T(8,128)(2,1)S(1)}, u32[]{:S(2)}, u32[]{:S(2)}) collective-permute-start(bf16[64,6144]{1,0:T(8,128)(2,1)S(1)} %get-tuple-element.37), channel_id=1, source_target_pairs={{0,1},{1,0},{2,3},{3,2},{4,5},{5,4},{6,7},{7,6},{8,9},{9,8},{10,11... | collective-permute-start | bytes 2359304 | tf_op jit(solution)/shard_map/ppermute | solution.py:24
  157.1 16.9 %collective-permute-start.15 = (bf16[64,6144]{1,0:T(8,128)(2,1)S(1)}, bf16[64,6144]{1,0:T(8,128)(2,1)S(1)}, u32[]{:S(2)}, u32[]{:S(2)}) collective-permute-start(bf16[64,6144]{1,0:T(8,128)(2,1)S(1)} %collective-permute-done.14), channel_id=1, source_target_pairs={{0,8},{1,33},{2,10},{3,35},{4,12},{5,37},{6,14},{7,39},{8,16},{9,4... | collective-permute-start | bytes 2359304 | tf_op jit(solution)/shard_map/ppermute | solution.py:24
  157.3 21.2 %collective-permute-start.37 = (bf16[64,6144]{1,0:T(8,128)(2,1)S(1)}, bf16[64,6144]{1,0:T(8,128)(2,1)S(1)}, u32[]{:S(2)}, u32[]{:S(2)}) collective-permute-start(bf16[64,6144]{1,0:T(8,128)(2,1)S(1)} %add_convert_fusion.1), channel_id=1, source_target_pairs={{0,24},{1,97},{2,26},{3,99},{4,28},{5,101},{6,30},{7,103},{8,0},{9... | collective-permute-start | bytes 2359304 | tf_op jit(solution)/shard_map/ppermute | solution.py:24
  165.5 16.9 %collective-permute-start.40 = (bf16[64,6144]{1,0:T(8,128)(2,1)S(1)}, bf16[64,6144]{1,0:T(8,128)(2,1)S(1)}, u32[]{:S(2)}, u32[]{:S(2)}) collective-permute-start(bf16[64,6144]{1,0:T(8,128)(2,1)S(1)} %add_convert_fusion), channel_id=1, source_target_pairs={{0,8},{1,33},{2,10},{3,35},{4,12},{5,37},{6,14},{7,39},{8,16},{9,4... | collective-permute-start | bytes 2359304 | tf_op jit(solution)/shard_map/ppermute | solution.py:24
  165.5 13.0 %collective-permute-start.30 = (bf16[64,6144]{1,0:T(8,128)(2,1)S(1)}, bf16[64,6144]{1,0:T(8,128)(2,1)S(1)}, u32[]{:S(2)}, u32[]{:S(2)}) collective-permute-start(bf16[64,6144]{1,0:T(8,128)(2,1)S(1)} %collective-permute-done.29), channel_id=1, source_target_pairs={{0,24},{1,97},{2,26},{3,99},{4,28},{5,101},{6,30},{7,103},{8,0},{9... | collective-permute-start | bytes 2359304 | tf_op jit(solution)/shard_map/ppermute | solution.py:24
  168.7 18.2 %collective-permute-start.27 = (bf16[64,6144]{1,0:T(8,128)(2,1)S(1)}, bf16[64,6144]{1,0:T(8,128)(2,1)S(1)}, u32[]{:S(2)}, u32[]{:S(2)}) collective-permute-start(bf16[64,6144]{1,0:T(8,128)(2,1)S(1)} %add_convert_fusion.3), channel_id=1, source_target_pairs={{0,24},{1,97},{2,26},{3,99},{4,28},{5,101},{6,30},{7,103},{8,0},{9... | collective-permute-start | bytes 2359304 | tf_op jit(solution)/shard_map/ppermute | solution.py:24
  173.9 16.9 %collective-permute-start.34 = (bf16[64,6144]{1,0:T(8,128)(2,1)S(1)}, bf16[64,6144]{1,0:T(8,128)(2,1)S(1)}, u32[]{:S(2)}, u32[]{:S(2)}) collective-permute-start(bf16[64,6144]{1,0:T(8,128)(2,1)S(1)} %add_convert_fusion.2), channel_id=1, source_target_pairs={{0,8},{1,33},{2,10},{3,35},{4,12},{5,37},{6,14},{7,39},{8,16},{9,4... | collective-permute-start | bytes 2359304 | tf_op jit(solution)/shard_map/ppermute | solution.py:24
  192.0 12.1 %collective-permute-start.41 = (bf16[64,6144]{1,0:T(8,128)(2,1)S(1)}, bf16[64,6144]{1,0:T(8,128)(2,1)S(1)}, u32[]{:S(2)}, u32[]{:S(2)}) collective-permute-start(bf16[64,6144]{1,0:T(8,128)(2,1)S(1)} %get-tuple-element.49), channel_id=1, source_target_pairs={{0,96},{1,25},{2,98},{3,27},{4,100},{5,29},{6,102},{7,31},{8,104},... | collective-permute-start | bytes 2359304 | tf_op jit(solution)/shard_map/ppermute | solution.py:24
  194.4 13.6 %collective-permute-start.42 = (bf16[64,6144]{1,0:T(8,128)(2,1)S(1)}, bf16[64,6144]{1,0:T(8,128)(2,1)S(1)}, u32[]{:S(2)}, u32[]{:S(2)}) collective-permute-start(bf16[64,6144]{1,0:T(8,128)(2,1)S(1)} %get-tuple-element.50), channel_id=1, source_target_pairs={{0,32},{1,9},{2,34},{3,11},{4,36},{5,13},{6,38},{7,15},{8,40},{9,1... | collective-permute-start | bytes 2359304 | tf_op jit(solution)/shard_map/ppermute | solution.py:24
  204.1 9.2 %collective-permute-start.43 = (bf16[32,6144]{1,0:T(8,128)(2,1)S(1)}, bf16[32,6144]{1,0:T(8,128)(2,1)S(1)}, u32[]{:S(2)}, u32[]{:S(2)}) collective-permute-start(bf16[32,6144]{1,0:T(8,128)(2,1)S(1)} %add_convert_fusion.5), channel_id=1, source_target_pairs={{0,96},{1,25},{2,98},{3,27},{4,100},{5,29},{6,102},{7,31},{8,104},... | collective-permute-start | bytes 1179656 | tf_op jit(solution)/shard_map/ppermute | solution.py:24
  208.1 9.1 %collective-permute-start.44 = (bf16[32,6144]{1,0:T(8,128)(2,1)S(1)}, bf16[32,6144]{1,0:T(8,128)(2,1)S(1)}, u32[]{:S(2)}, u32[]{:S(2)}) collective-permute-start(bf16[32,6144]{1,0:T(8,128)(2,1)S(1)} %add_convert_fusion.4), channel_id=1, source_target_pairs={{0,32},{1,9},{2,34},{3,11},{4,36},{5,13},{6,38},{7,15},{8,40},{9,1... | collective-permute-start | bytes 1179656 | tf_op jit(solution)/shard_map/ppermute | solution.py:24
  226.7 9.7 %collective-permute-start.46 = (bf16[128,768]{1,0:T(8,128)(2,1)S(1)}, bf16[128,768]{1,0:T(8,128)(2,1)S(1)}, u32[]{:S(2)}, u32[]{:S(2)}) collective-permute-start(bf16[128,768]{1,0:T(8,128)(2,1)S(1)} %get-tuple-element.56), channel_id=1, source_target_pairs={{0,4},{1,5},{2,6},{3,7},{4,0},{5,1},{6,2},{7,3},{8,12},{9,13},{10,... | collective-permute-start | bytes 589832 | tf_op jit(solution)/shard_map/ppermute | solution.py:24
  230.6 9.4 %collective-permute-start.47 = (bf16[128,768]{1,0:T(8,128)(2,1)S(1)}, bf16[128,768]{1,0:T(8,128)(2,1)S(1)}, u32[]{:S(2)}, u32[]{:S(2)}) collective-permute-start(bf16[128,768]{1,0:T(8,128)(2,1)S(1)} %get-tuple-element.57), channel_id=1, source_target_pairs={{0,2},{1,3},{2,4},{3,5},{4,6},{5,7},{6,0},{7,1},{8,10},{9,11},{10,... | collective-permute-start | bytes 589832 | tf_op jit(solution)/shard_map/ppermute | solution.py:24
  231.7 9.1 %collective-permute-start.48 = (bf16[128,768]{1,0:T(8,128)(2,1)S(1)}, bf16[128,768]{1,0:T(8,128)(2,1)S(1)}, u32[]{:S(2)}, u32[]{:S(2)}) collective-permute-start(bf16[128,768]{1,0:T(8,128)(2,1)S(1)} %get-tuple-element.58), channel_id=1, source_target_pairs={{0,6},{1,7},{2,0},{3,1},{4,2},{5,3},{6,4},{7,5},{8,14},{9,15},{10,... | collective-permute-start | bytes 589832 | tf_op jit(solution)/shard_map/ppermute | solution.py:24
  (17 other events, 256.9 us)

commit v2 on v1

--- a/solution.py
+++ b/solution.py
@@ -81,44 +81,40 @@
     )(*args)
 
 
-def line_kernel(*refs):
-    chains, (minus, plus, near_minus, near_plus, own) = (refs[:6], refs[6:12]), refs[12:]
+def line_kernel(own_low, low_before, from_after, own_high, low_after, from_before, *outs):
+    minus, plus, near_minus, near_plus, own = outs
     tile = 512
-    q = near_minus.shape[0] // 2
+    q = near_minus.shape[0]
 
     @pl.loop(0, minus.shape[1] // tile)
     def _(i):
         at = pl.ds(pl.multiple_of(i * tile, tile), tile)
-        for k, (own_low, low_before, from_after, own_high, low_after, from_before) in enumerate(chains):
-            low = add(own_low[:, at], low_before[:, at], from_after[:, at])
-            high = add(own_high[:, at], low_after[:, at], from_before[:, at])
-
-            def put(out, row, value):
-                out[pl.ds(row + k * q, q), at] = value.astype(out.dtype)
-
-            put(own, 0, low[:q])
-            put(own, 2 * q, low[q:2 * q])
-            put(near_minus, 0, low[2 * q:3 * q])
-            put(minus, 2 * q, low[3 * q:])
-            put(plus, 2 * q, high[:q])
-            put(near_plus, 0, high[q:2 * q])
-            put(minus, 0, high[2 * q:3 * q])
-            put(plus, 0, high[3 * q:])
-
-
-def sum_kernel(place, own, from_minus, from_plus, near_after, near_before, mine, theirs):
-    half = near_after.shape[0]
-    q = half // 2
+        low = add(own_low[:, at], low_before[:, at], from_after[:, at])
+        high = add(own_high[:, at], low_after[:, at], from_before[:, at])
+        own[:, at] = low[:2 * q]
+        near_minus[:, at] = low[2 * q:3 * q]
+        minus[q:, at] = low[3 * q:].astype(BF16)
+        plus[q:, at] = high[:q].astype(BF16)
+        near_plus[:, at] = high[q:2 * q]
+        minus[:q, at] = high[2 * q:3 * q].astype(BF16)
+        plus[:q, at] = high[3 * q:].astype(BF16)
+
+
+def sum_kernel(place, *refs):
+    chains, (mine, theirs) = (refs[:5], refs[5:10]), refs[10:]
     width = mine.shape[1] // SIDE
+    q = mine.shape[0] // 4
 
     @pl.loop(0, SIDE)
     def _(k):
         to = pl.ds(pl.multiple_of(k * width, width), width)
         for core, out in ((place[1], mine), (1 - place[1], theirs)):
             at = pl.ds(pl.multiple_of((CORES * k + core) * width, width), width)
-            first = add(own[:half, at], from_plus[half:, at], near_after[:, at]).astype(BF16)
-            second = add(own[half:, at], from_minus[half:, at], near_before[:, at]).astype(BF16)
-            out[:, to] = jnp.concatenate([first[:q], second[:q], first[q:], second[q:]], 0)
+            for n, (own, from_minus, from_plus, near_after, near_before) in enumerate(chains):
+                first = add(own[:q, at], from_plus[q:, at], near_after[:, at])
+                second = add(own[q:, at], from_minus[q:, at], near_before[:, at])
+                rows = pl.ds(2 * n * q, 2 * q)
+                out[rows, to] = jnp.concatenate([first, second], 0).astype(BF16)
 
 
 def spread_kernel(place, mine, theirs, picks, weights, *outs):
@@ -260,16 +256,21 @@
 
     width = tokens.shape[1]
     q = half // 2
-    minus, plus, near_minus, near_plus, own_sum = vmem_call(
-        line_kernel,
-        [((4 * q, width), BF16)] * 2 + [((2 * q, width), F32)] * 2 + [((4 * q, width), F32)],
-        *scatter(back["pl"], back["pn"], back["pf"]),
-        *scatter(line[:2], near_own, far[:2]),
-    )
-    from_minus = hop(minus, 0, -1)
-    from_plus = hop(plus, 0, 1)
-    near_after = hop(add(near_minus, from_minus[:2 * q]).astype(BF16), 0, -1)
-    near_before = hop(add(near_plus, from_plus[:2 * q]).astype(BF16), 0, 1)
+
+    def second_leg(terms):
+        minus, plus, near_minus, near_plus, own_sum = vmem_call(
+            line_kernel,
+            [((2 * q, width), BF16)] * 2 + [((q, width), F32)] * 2 + [((2 * q, width), F32)],
+            *terms,
+        )
+        from_minus = hop(minus, 0, -1)
+        from_plus = hop(plus, 0, 1)
+        near_after = hop(add(near_minus, from_minus[:q]).astype(BF16), 0, -1)
+        near_before = hop(add(near_plus, from_plus[:q]).astype(BF16), 0, 1)
+        return own_sum, from_minus, from_plus, near_after, near_before
+
+    own_terms = second_leg(scatter(line[:2], near_own, far[:2]))
+    other_terms = second_leg(scatter(back["pl"], back["pn"], back["pf"]))
 
     part = width // experts
     picks = jnp.stack([pick_other.T, pick_own.T])
@@ -278,7 +279,7 @@
     mine, theirs = vmem_call(
         sum_kernel,
         [((slots, SIDE * part), BF16)] * 2,
-        place, own_sum, from_minus, from_plus, near_after, near_before,
+        place, *other_terms, *own_terms,
         scalars=1,
     )
     sums = vmem_call(
@@ -301,4 +302,6 @@
         P("expert", None, "dp"),
         P("expert", "dp", None),
     )
-    return jax.shard_map(layer, mesh=mesh, in_specs=in_specs, out_specs=P("dp", "expert"), check_vma=False)
+    return jax.shard_map(
+        layer, mesh=mesh, in_specs=in_specs, out_specs=P("dp", "expert"), check_vma=False
+    )

time: 242 us -> 236 us (0.975)
  waiting for transfers between devices: 134 us -> 110 us
  local copies, waits for them, and re-layouts: 9.05 us -> 16.6 us
  starting transfers between devices: 57 us -> 62.7 us
  other arithmetic: 5.72 us -> 8.63 us
    ppermute x49 -> x53, waiting for transfers between devices: 134 us -> 110 us  [move(): return lax.ppermute(value, ('dp', 'expert'), pairs)]
    unnamed x38 -> x48, local copies, waits for them, and re-layouts: 8.27 us -> 15.8 us
    ppermute x49 -> x53, starting transfers between devices: 57 us -> 62.7 us  [move(): return lax.ppermute(value, ('dp', 'expert'), pairs)]
    pallas_call x4 -> x5, Pallas kernels: 4.66 us -> 5.42 us  [vmem_call(): pl.pallas_call(kernel, in_specs=specs, out_specs=[space] * len(outs), out...]
  transfers between devices with their start and end apart: 49 -> 53, of which waited for: 24 -> 24; matrix products, arithmetic and copies ran while one was open for 1% -> 2% of each run, Pallas kernels for 13% -> 11%
where the time goes in v2:
time: 236 us
  waiting for transfers between devices  110 us (47%)
  starting transfers between devices  62.7 us (27%)
  Pallas kernels  36.7 us (16%)
  local copies, waits for them, and re-layouts  16.6 us (7%)
  other arithmetic  8.63 us (4%)
    ppermute x53, waiting for transfers between devices, move(): return lax.ppermute(value, ('dp', 'expert'), pairs)  110 us
    ppermute x53, starting transfers between devices, move(): return lax.ppermute(value, ('dp', 'expert'), pairs)  62.7 us
    pallas_call x4, Pallas kernels, ffn(): pl.pallas_call(lambda *refs: ffn_kernel(len(sizes), *refs), name='ffn', g...  31.3 us
    unnamed x48, local copies, waits for them, and re-layouts  15.8 us
    pallas_call x5, Pallas kernels, vmem_call(): pl.pallas_call(kernel, in_specs=specs, out_specs=[space] * len(outs), out...  5.42 us
  transfers between devices with their start and end apart: 53, of which 24 were waited for; matrix products, arithmetic and copies ran while one was open for 2% of the time, Pallas kernels for 11%

profile of v2, /device:TPU:0, one launch (start us, length us, event | category | flops | bytes accessed | tf_op | source)
XLA Modules:
  0.0 235.9 jit_solution(14077086747713321230)
XLA Ops:
  5.1 1.7 collective-permute-start
  6.7 1.6 collective-permute-start.1
  8.8 2.9 %collective-permute-start.5 = (bf16[32,6144]{1,0:T(8,128)(2,1)S(1)}, bf16[32,6144]{1,0:T(8,128)(2,1)S(1)}, u32[]{:S(2)}, u32[]{:S(2)}) collective-permute-start(bf16[32,6144]{1,0:T(8,128)(2,1)S(1)} %get-tuple-element.75), channel_id=1, source_target_pairs={{0,96},{1,25},{2,98},{3,27},{4,100},{5,29},{6,102},{7,31},{8,104},... | collective-permute-start | bytes 1179656 | tf_op jit(solution)/shard_map/ppermute | solution.py:24
  11.6 2.5 %collective-permute-done = bf16[32,6144]{1,0:T(8,128)(2,1)S(1)} collective-permute-done((bf16[32,6144]{1,0:T(8,128)(2,1)S(1)}, bf16[32,6144]{1,0:T(8,128)(2,1)S(1)}, u32[]{:S(2)}, u32[]{:S(2)}) %collective-permute-start) | collective-permute-done | bytes 393248 | tf_op jit(solution)/shard_map/ppermute | solution.py:24
  14.6 2.9 %collective-permute-start.3 = (bf16[16,6144]{1,0:T(8,128)(2,1)S(1)}, bf16[16,6144]{1,0:T(8,128)(2,1)S(1)}, u32[]{:S(2)}, u32[]{:S(2)}) collective-permute-start(bf16[16,6144]{1,0:T(8,128)(2,1)S(1)} %slice.70), channel_id=1, source_target_pairs={{0,96},{1,25},{2,98},{3,27},{4,100},{5,29},{6,102},{7,31},{8,104},... | collective-permute-start | bytes 589832 | tf_op jit(solution)/shard_map/ppermute | solution.py:24
  18.8 2.9 %collective-permute-start.7 = (bf16[16,6144]{1,0:T(8,128)(2,1)S(1)}, bf16[16,6144]{1,0:T(8,128)(2,1)S(1)}, u32[]{:S(2)}, u32[]{:S(2)}) collective-permute-start(bf16[16,6144]{1,0:T(8,128)(2,1)S(1)} %slice.73), channel_id=1, source_target_pairs={{0,96},{1,25},{2,98},{3,27},{4,100},{5,29},{6,102},{7,31},{8,104},... | collective-permute-start | bytes 589832 | tf_op jit(solution)/shard_map/ppermute | solution.py:24
  21.9 3.4 %collective-permute-done.6 = bf16[16,6144]{1,0:T(8,128)(2,1)S(1)} collective-permute-done((bf16[16,6144]{1,0:T(8,128)(2,1)S(1)}, bf16[16,6144]{1,0:T(8,128)(2,1)S(1)}, u32[]{:S(2)}, u32[]{:S(2)}) %collective-permute-start.6) | collective-permute-done | bytes 196640 | tf_op jit(solution)/shard_map/ppermute | solution.py:24
  25.4 1.8 collective-permute-start.10
  27.1 1.6 collective-permute-start.12
  29.3 2.8 %collective-permute-start.19 = (bf16[128,6144]{1,0:T(8,128)(2,1)S(1)}, bf16[128,6144]{1,0:T(8,128)(2,1)S(1)}, u32[]{:S(2)}, u32[]{:S(2)}) collective-permute-start(bf16[128,6144]{1,0:T(8,128)(2,1)S(1)} %constant_dynamic-update-slice_fusion.refs_0_), channel_id=1, source_target_pairs={{0,24},{1,97},{2,26},{3,99},{4,28},{5,101},{6,30},{7,103},{8,0},{9... | collective-permute-start | bytes 4718600 | tf_op jit(solution)/shard_map/ppermute | solution.py:24
  32.0 15.0 %collective-permute-done.10 = bf16[128,6144]{1,0:T(8,128)(2,1)S(1)} collective-permute-done((bf16[128,6144]{1,0:T(8,128)(2,1)S(1)}, bf16[128,6144]{1,0:T(8,128)(2,1)S(1)}, u32[]{:S(2)}, u32[]{:S(2)}) %collective-permute-start.10) | collective-permute-done | bytes 1572896 | tf_op jit(solution)/shard_map/ppermute | solution.py:24
  47.7 2.8 %collective-permute-start.23 = (bf16[64,6144]{1,0:T(8,128)(2,1)S(1)}, bf16[64,6144]{1,0:T(8,128)(2,1)S(1)}, u32[]{:S(2)}, u32[]{:S(2)}) collective-permute-start(bf16[64,6144]{1,0:T(8,128)(2,1)S(1)} %slice.77), channel_id=1, source_target_pairs={{0,24},{1,97},{2,26},{3,99},{4,28},{5,101},{6,30},{7,103},{8,0},{9... | collective-permute-start | bytes 2359304 | tf_op jit(solution)/shard_map/ppermute | solution.py:24
  50.5 13.4 %collective-permute-done.17.refs_0_ = bf16[128,6144]{1,0:T(8,128)(2,1)S(1)} collective-permute-done((bf16[128,6144]{1,0:T(8,128)(2,1)S(1)}, bf16[128,6144]{1,0:T(8,128)(2,1)S(1)}, u32[]{:S(2)}, u32[]{:S(2)}) %collective-permute-start.17) | collective-permute-done | bytes 1572896 | tf_op jit(solution)/shard_map/ppermute | solution.py:24
  64.6 2.8 %collective-permute-start.20 = (bf16[64,6144]{1,0:T(8,128)(2,1)S(1)}, bf16[64,6144]{1,0:T(8,128)(2,1)S(1)}, u32[]{:S(2)}, u32[]{:S(2)}) collective-permute-start(bf16[64,6144]{1,0:T(8,128)(2,1)S(1)} %slice.75), channel_id=1, source_target_pairs={{0,24},{1,97},{2,26},{3,99},{4,28},{5,101},{6,30},{7,103},{8,0},{9... | collective-permute-start | bytes 2359304 | tf_op jit(solution)/shard_map/ppermute | solution.py:24
  67.4 4.9 %collective-permute-done.21 = bf16[64,6144]{1,0:T(8,128)(2,1)S(1)} collective-permute-done((bf16[64,6144]{1,0:T(8,128)(2,1)S(1)}, bf16[64,6144]{1,0:T(8,128)(2,1)S(1)}, u32[]{:S(2)}, u32[]{:S(2)}) %collective-permute-start.21) | collective-permute-done | bytes 786464 | tf_op jit(solution)/shard_map/ppermute | solution.py:24
  72.8 7.9 %collective-permute-done.18.refs_0_ = bf16[64,6144]{1,0:T(8,128)(2,1)S(1)} collective-permute-done((bf16[64,6144]{1,0:T(8,128)(2,1)S(1)}, bf16[64,6144]{1,0:T(8,128)(2,1)S(1)}, u32[]{:S(2)}, u32[]{:S(2)}) %collective-permute-start.18) | collective-permute-done | bytes 786464 | tf_op jit(solution)/shard_map/ppermute | solution.py:24
  81.3 2.8 %copy-done.5 = bf16[1,512,6144]{2,1,0:T(8,128)(2,1)S(1)} copy-done((bf16[1,512,6144]{2,1,0:T(8,128)(2,1)S(1)}, bf16[1,512,6144]{2,1,0:T(8,128)(2,1)}, u32[]{:S(2)}) %copy-start.5) | copy-done | bytes 6291480
  84.1 8.2 %ffn.6 = (bf16[64,6144]{1,0:T(8,128)(2,1)S(1)}, bf16[64,6144]{1,0:T(8,128)(2,1)S(1)}, bf16[64,6144]{1,0:T(8,128)(2,1)S(1)}, bf16[64,6144]{1,0:T(8,128)(2,1)}) custom-call(bf16[64,6144]{1,0:T(8,128)(2,1)S(1)} %collective-permute-done.18.refs_0_, bf16[64,6144]{1,0:T(8,128)(2,1)S(1)} %collective-permute-done.20.refs_1_, ...), custom_call_target="tpu_custom_call" | custom-call | flops 4831838208 | bytes 25165824 | tf_op jit(solution)/shard_map/ffn/pallas_call | solution.py:188
  92.3 2.8 %collective-permute-start.40 = (bf16[64,6144]{1,0:T(8,128)(2,1)S(1)}, bf16[64,6144]{1,0:T(8,128)(2,1)S(1)}, u32[]{:S(2)}, u32[]{:S(2)}) collective-permute-start(bf16[64,6144]{1,0:T(8,128)(2,1)S(1)} %get-tuple-element.53), channel_id=1, source_target_pairs={{0,24},{1,97},{2,26},{3,99},{4,28},{5,101},{6,30},{7,103},{8,0},{9... | collective-permute-start | bytes 2359304 | tf_op jit(solution)/shard_map/ppermute | solution.py:24
  95.1 7.5 %ffn.7 = (bf16[64,6144]{1,0:T(8,128)(2,1)S(1)}, bf16[64,6144]{1,0:T(8,128)(2,1)S(1)}, bf16[64,6144]{1,0:T(8,128)(2,1)S(1)}, bf16[64,6144]{1,0:T(8,128)(2,1)S(1)}) custom-call(bf16[128,6144]{1,0:T(8,128)(2,1)S(1)} %collective-permute-done.17.refs_0_, bf16[128,6144]{1,0:T(8,128)(2,1)S(1)} %collective-permute-done.19.refs_1_, ...), custom_call_target="tpu_custom_call" | custom-call | flops 4831838208 | bytes 25165824 | tf_op jit(solution)/shard_map/ffn/pallas_call | solution.py:188
  107.0 2.4 %collective-permute-start.42 = (bf16[64,6144]{1,0:T(8,128)(2,1)S(1)}, bf16[64,6144]{1,0:T(8,128)(2,1)S(1)}, u32[]{:S(2)}, u32[]{:S(2)}) collective-permute-start(bf16[64,6144]{1,0:T(8,128)(2,1)S(1)} %get-tuple-element.55), channel_id=1, source_target_pairs={{0,24},{1,97},{2,26},{3,99},{4,28},{5,101},{6,30},{7,103},{8,0},{9... | collective-permute-start | bytes 2359304 | tf_op jit(solution)/shard_map/ppermute | solution.py:24
  109.4 14.8 %collective-permute-done.43 = bf16[64,6144]{1,0:T(8,128)(2,1)S(1)} collective-permute-done((bf16[64,6144]{1,0:T(8,128)(2,1)S(1)}, bf16[64,6144]{1,0:T(8,128)(2,1)S(1)}, u32[]{:S(2)}, u32[]{:S(2)}) %collective-permute-start.43) | collective-permute-done | bytes 786464 | tf_op jit(solution)/shard_map/ppermute | solution.py:24
  125.8 1.6 collective-permute-start.44
  127.4 8.1 %ffn.5 = (bf16[64,6144]{1,0:T(8,128)(2,1)}, bf16[64,6144]{1,0:T(8,128)(2,1)S(1)}, bf16[64,6144]{1,0:T(8,128)(2,1)S(1)}, bf16[64,6144]{1,0:T(8,128)(2,1)S(1)}) custom-call(bf16[128,6144]{1,0:T(8,128)(2,1)S(1)} %collective-permute-done.11.refs_0_, bf16[128,6144]{1,0:T(8,128)(2,1)S(1)} %collective-permute-done.13.refs_1_, bf16[1,6144,512]{2,1,0:T(8,128)(2,1)S(1)} %bitcast.11, ...), custom_call_target="tpu_custom_call" | custom-call | flops 4831838208 | bytes 25165824 | tf_op jit(solution)/shard_map/ffn/pallas_call | solution.py:188
  139.0 1.5 collective-permute-start.16
  142.0 2.8 %copy-done.2 = bf16[1,6144,512]{2,1,0:T(8,128)(2,1)S(1)} copy-done((bf16[1,6144,512]{2,1,0:T(8,128)(2,1)S(1)}, bf16[1,6144,512]{2,1,0:T(8,128)(2,1)}, u32[]{:S(2)}) %copy-start.2) | copy-done | bytes 6291480
  144.8 2.8 %copy-done.4 = bf16[1,6144,512]{2,1,0:T(8,128)(2,1)S(1)} copy-done((bf16[1,6144,512]{2,1,0:T(8,128)(2,1)S(1)}, bf16[1,6144,512]{2,1,0:T(8,128)(2,1)}, u32[]{:S(2)}) %copy-start.4) | copy-done | bytes 6291480
  147.6 2.8 %copy-done.6 = bf16[1,512,6144]{2,1,0:T(8,128)(2,1)S(1)} copy-done((bf16[1,512,6144]{2,1,0:T(8,128)(2,1)S(1)}, bf16[1,512,6144]{2,1,0:T(8,128)(2,1)}, u32[]{:S(2)}) %copy-start.6) | copy-done | bytes 6291480
  150.4 7.5 %ffn.4 = (bf16[64,6144]{1,0:T(8,128)(2,1)S(1)}, bf16[64,6144]{1,0:T(8,128)(2,1)S(1)}, bf16[64,6144]{1,0:T(8,128)(2,1)S(1)}, bf16[64,6144]{1,0:T(8,128)(2,1)S(1)}) custom-call(bf16[128,6144]{1,0:T(8,128)(2,1)S(1)} %constant_dynamic-update-slice_fusion.refs_0_, bf16[128,6144]{1,0:T(8,128)(2,1)S(1)} %collective-permute-done.8.refs_1_, ...), custom_call_target="tpu_custom_call" | custom-call | flops 4831838208 | bytes 25165824 | tf_op jit(solution)/shard_map/ffn/pallas_call | solution.py:188
  157.9 2.6 %collective-permute-start.9 = (bf16[64,6144]{1,0:T(8,128)(2,1)S(1)}, bf16[64,6144]{1,0:T(8,128)(2,1)S(1)}, u32[]{:S(2)}, u32[]{:S(2)}) collective-permute-start(bf16[64,6144]{1,0:T(8,128)(2,1)S(1)} %get-tuple-element.37), channel_id=1, source_target_pairs={{0,1},{1,0},{2,3},{3,2},{4,5},{5,4},{6,7},{7,6},{8,9},{9,8},{10,11... | collective-permute-start | bytes 2359304 | tf_op jit(solution)/shard_map/ppermute | solution.py:24
  160.7 2.1 shard_map.74
  163.4 1.6 add_convert_fusion.3
  166.3 2.4 %collective-permute-start.30 = (bf16[64,6144]{1,0:T(8,128)(2,1)S(1)}, bf16[64,6144]{1,0:T(8,128)(2,1)S(1)}, u32[]{:S(2)}, u32[]{:S(2)}) collective-permute-start(bf16[64,6144]{1,0:T(8,128)(2,1)S(1)} %collective-permute-done.29), channel_id=1, source_target_pairs={{0,24},{1,97},{2,26},{3,99},{4,28},{5,101},{6,30},{7,103},{8,0},{9... | collective-permute-start | bytes 2359304 | tf_op jit(solution)/shard_map/ppermute | solution.py:24
  168.7 8.1 %collective-permute-done.33 = bf16[64,6144]{1,0:T(8,128)(2,1)S(1)} collective-permute-done((bf16[64,6144]{1,0:T(8,128)(2,1)}, bf16[64,6144]{1,0:T(8,128)(2,1)S(1)}, u32[]{:S(2)}, u32[]{:S(2)}) %collective-permute-start.33) | collective-permute-done | bytes 786464 | tf_op jit(solution)/shard_map/ppermute | solution.py:24
  177.9 2.0 collective-permute-start.34
  179.9 8.9 %collective-permute-done.45.refs_6_ = bf16[32,6144]{1,0:T(8,128)(2,1)S(1)} collective-permute-done((bf16[32,6144]{1,0:T(8,128)(2,1)S(1)}, bf16[32,6144]{1,0:T(8,128)(2,1)S(1)}, u32[]{:S(2)}, u32[]{:S(2)}) %collective-permute-start.45) | collective-permute-done | bytes 393248 | tf_op jit(solution)/shard_map/ppermute | solution.py:24
  188.8 3.3 %collective-permute-start.47 = (bf16[16,6144]{1,0:T(8,128)(2,1)S(1)}, bf16[16,6144]{1,0:T(8,128)(2,1)S(1)}, u32[]{:S(2)}, u32[]{:S(2)}) collective-permute-start(bf16[16,6144]{1,0:T(8,128)(2,1)S(1)} %add_convert_fusion.5), channel_id=1, source_target_pairs={{0,96},{1,25},{2,98},{3,27},{4,100},{5,29},{6,102},{7,31},{8,104},... | collective-permute-start | bytes 589832 | tf_op jit(solution)/shard_map/ppermute | solution.py:24
  192.1 1.5 collective-permute-done.27.from_after
  193.7 3.8 %collective-permute-done.34.from_before = bf16[64,6144]{1,0:T(8,128)(2,1)S(1)} collective-permute-done((bf16[64,6144]{1,0:T(8,128)(2,1)S(1)}, bf16[64,6144]{1,0:T(8,128)(2,1)S(1)}, u32[]{:S(2)}, u32[]{:S(2)}) %collective-permute-start.34) | collective-permute-done | bytes 786464 | tf_op jit(solution)/shard_map/ppermute | solution.py:24
  198.7 1.8 collective-permute-start.48
  200.6 5.3 %collective-permute-done.35.refs_1_ = bf16[32,6144]{1,0:T(8,128)(2,1)S(1)} collective-permute-done((bf16[32,6144]{1,0:T(8,128)(2,1)S(1)}, bf16[32,6144]{1,0:T(8,128)(2,1)S(1)}, u32[]{:S(2)}, u32[]{:S(2)}) %collective-permute-start.35) | collective-permute-done | bytes 393248 | tf_op jit(solution)/shard_map/ppermute | solution.py:24
  206.0 1.8 collective-permute-start.37
  207.8 2.3 collective-permute-done.36.refs_2_
  211.7 5.4 %collective-permute-done.38.refs_4_ = bf16[16,6144]{1,0:T(8,128)(2,1)S(1)} collective-permute-done((bf16[16,6144]{1,0:T(8,128)(2,1)S(1)}, bf16[16,6144]{1,0:T(8,128)(2,1)S(1)}, u32[]{:S(2)}, u32[]{:S(2)}) %collective-permute-start.38) | collective-permute-done | bytes 196640 | tf_op jit(solution)/shard_map/ppermute | solution.py:24
  220.9 4.1 %collective-permute-start.50 = (bf16[128,768]{1,0:T(8,128)(2,1)S(1)}, bf16[128,768]{1,0:T(8,128)(2,1)S(1)}, u32[]{:S(2)}, u32[]{:S(2)}) collective-permute-start(bf16[128,768]{1,0:T(8,128)(2,1)S(1)} %get-tuple-element.66), channel_id=1, source_target_pairs={{0,4},{1,5},{2,6},{3,7},{4,0},{5,1},{6,2},{7,3},{8,12},{9,13},{10,... | collective-permute-start | bytes 589832 | tf_op jit(solution)/shard_map/ppermute | solution.py:24
  225.9 2.2 collective-permute-start.52
  228.2 2.5 %collective-permute-done.50.refs_0_ = bf16[128,768]{1,0:T(8,128)(2,1)S(1)} collective-permute-done((bf16[128,768]{1,0:T(8,128)(2,1)S(1)}, bf16[128,768]{1,0:T(8,128)(2,1)S(1)}, u32[]{:S(2)}, u32[]{:S(2)}) %collective-permute-start.50) | collective-permute-done | bytes 196640 | tf_op jit(solution)/shard_map/ppermute | solution.py:24
  230.7 3.7 %collective-permute-done.51.refs_1_ = bf16[128,768]{1,0:T(8,128)(2,1)S(1)} collective-permute-done((bf16[128,768]{1,0:T(8,128)(2,1)S(1)}, bf16[128,768]{1,0:T(8,128)(2,1)S(1)}, u32[]{:S(2)}, u32[]{:S(2)}) %collective-permute-start.51) | collective-permute-done | bytes 196640 | tf_op jit(solution)/shard_map/ppermute | solution.py:24
  (156 shorter events, 33.6 us)
Async XLA Ops:
  5.1 9.1 %collective-permute-start = (bf16[32,6144]{1,0:T(8,128)(2,1)S(1)}, bf16[32,6144]{1,0:T(8,128)(2,1)S(1)}, u32[]{:S(2)}, u32[]{:S(2)}) collective-permute-start(bf16[32,6144]{1,0:T(8,128)(2,1)S(1)} %get-tuple-element.78), channel_id=1, source_target_pairs={{0,32},{1,9},{2,34},{3,11},{4,36},{5,13},{6,38},{7,15},{8,40},{9,1... | collective-permute-start | bytes 1179656 | tf_op jit(solution)/shard_map/ppermute | solution.py:24
  6.7 7.9 %collective-permute-start.1 = (bf16[32,6144]{1,0:T(8,128)(2,1)S(1)}, bf16[32,6144]{1,0:T(8,128)(2,1)S(1)}, u32[]{:S(2)}, u32[]{:S(2)}) collective-permute-start(bf16[32,6144]{1,0:T(8,128)(2,1)S(1)} %get-tuple-element.78), channel_id=1, source_target_pairs={{0,96},{1,25},{2,98},{3,27},{4,100},{5,29},{6,102},{7,31},{8,104},... | collective-permute-start | bytes 1179656 | tf_op jit(solution)/shard_map/ppermute | solution.py:24
  8.4 10.0 %collective-permute-start.4 = (bf16[32,6144]{1,0:T(8,128)(2,1)S(1)}, bf16[32,6144]{1,0:T(8,128)(2,1)S(1)}, u32[]{:S(2)}, u32[]{:S(2)}) collective-permute-start(bf16[32,6144]{1,0:T(8,128)(2,1)S(1)} %get-tuple-element.75), channel_id=1, source_target_pairs={{0,32},{1,9},{2,34},{3,11},{4,36},{5,13},{6,38},{7,15},{8,40},{9,1... | collective-permute-start | bytes 1179656 | tf_op jit(solution)/shard_map/ppermute | solution.py:24
  8.8 10.1 %collective-permute-start.5 = (bf16[32,6144]{1,0:T(8,128)(2,1)S(1)}, bf16[32,6144]{1,0:T(8,128)(2,1)S(1)}, u32[]{:S(2)}, u32[]{:S(2)}) collective-permute-start(bf16[32,6144]{1,0:T(8,128)(2,1)S(1)} %get-tuple-element.75), channel_id=1, source_target_pairs={{0,96},{1,25},{2,98},{3,27},{4,100},{5,29},{6,102},{7,31},{8,104},... | collective-permute-start | bytes 1179656 | tf_op jit(solution)/shard_map/ppermute | solution.py:24
  14.1 14.5 %collective-permute-start.2 = (bf16[16,6144]{1,0:T(8,128)(2,1)S(1)}, bf16[16,6144]{1,0:T(8,128)(2,1)S(1)}, u32[]{:S(2)}, u32[]{:S(2)}) collective-permute-start(bf16[16,6144]{1,0:T(8,128)(2,1)S(1)} %slice.69), channel_id=1, source_target_pairs={{0,32},{1,9},{2,34},{3,11},{4,36},{5,13},{6,38},{7,15},{8,40},{9,1... | collective-permute-start | bytes 589832 | tf_op jit(solution)/shard_map/ppermute | solution.py:24
  14.6 14.1 %collective-permute-start.3 = (bf16[16,6144]{1,0:T(8,128)(2,1)S(1)}, bf16[16,6144]{1,0:T(8,128)(2,1)S(1)}, u32[]{:S(2)}, u32[]{:S(2)}) collective-permute-start(bf16[16,6144]{1,0:T(8,128)(2,1)S(1)} %slice.70), channel_id=1, source_target_pairs={{0,96},{1,25},{2,98},{3,27},{4,100},{5,29},{6,102},{7,31},{8,104},... | collective-permute-start | bytes 589832 | tf_op jit(solution)/shard_map/ppermute | solution.py:24
  18.4 6.9 %collective-permute-start.6 = (bf16[16,6144]{1,0:T(8,128)(2,1)S(1)}, bf16[16,6144]{1,0:T(8,128)(2,1)S(1)}, u32[]{:S(2)}, u32[]{:S(2)}) collective-permute-start(bf16[16,6144]{1,0:T(8,128)(2,1)S(1)} %slice.72), channel_id=1, source_target_pairs={{0,32},{1,9},{2,34},{3,11},{4,36},{5,13},{6,38},{7,15},{8,40},{9,1... | collective-permute-start | bytes 589832 | tf_op jit(solution)/shard_map/ppermute | solution.py:24
  18.8 6.5 %collective-permute-start.7 = (bf16[16,6144]{1,0:T(8,128)(2,1)S(1)}, bf16[16,6144]{1,0:T(8,128)(2,1)S(1)}, u32[]{:S(2)}, u32[]{:S(2)}) collective-permute-start(bf16[16,6144]{1,0:T(8,128)(2,1)S(1)} %slice.73), channel_id=1, source_target_pairs={{0,96},{1,25},{2,98},{3,27},{4,100},{5,29},{6,102},{7,31},{8,104},... | collective-permute-start | bytes 589832 | tf_op jit(solution)/shard_map/ppermute | solution.py:24
  25.4 21.7 %collective-permute-start.10 = (bf16[128,6144]{1,0:T(8,128)(2,1)S(1)}, bf16[128,6144]{1,0:T(8,128)(2,1)S(1)}, u32[]{:S(2)}, u32[]{:S(2)}) collective-permute-start(bf16[128,6144]{1,0:T(8,128)(2,1)S(1)} %constant_dynamic-update-slice_fusion.5), channel_id=1, source_target_pairs={{0,8},{1,33},{2,10},{3,35},{4,12},{5,37},{6,14},{7,39},{8,16},{9,4... | collective-permute-start | bytes 4718600 | tf_op jit(solution)/shard_map/ppermute | solution.py:24
  27.1 20.5 %collective-permute-start.12 = (bf16[128,6144]{1,0:T(8,128)(2,1)S(1)}, bf16[128,6144]{1,0:T(8,128)(2,1)S(1)}, u32[]{:S(2)}, u32[]{:S(2)}) collective-permute-start(bf16[128,6144]{1,0:T(8,128)(2,1)S(1)} %constant_dynamic-update-slice_fusion.5), channel_id=1, source_target_pairs={{0,24},{1,97},{2,26},{3,99},{4,28},{5,101},{6,30},{7,103},{8,0},{9... | collective-permute-start | bytes 4718600 | tf_op jit(solution)/shard_map/ppermute | solution.py:24
  28.7 35.2 %collective-permute-start.17 = (bf16[128,6144]{1,0:T(8,128)(2,1)S(1)}, bf16[128,6144]{1,0:T(8,128)(2,1)S(1)}, u32[]{:S(2)}, u32[]{:S(2)}) collective-permute-start(bf16[128,6144]{1,0:T(8,128)(2,1)S(1)} %constant_dynamic-update-slice_fusion.refs_0_), channel_id=1, source_target_pairs={{0,8},{1,33},{2,10},{3,35},{4,12},{5,37},{6,14},{7,39},{8,16},{9,4... | collective-permute-start | bytes 4718600 | tf_op jit(solution)/shard_map/ppermute | solution.py:24
  29.3 35.2 %collective-permute-start.19 = (bf16[128,6144]{1,0:T(8,128)(2,1)S(1)}, bf16[128,6144]{1,0:T(8,128)(2,1)S(1)}, u32[]{:S(2)}, u32[]{:S(2)}) collective-permute-start(bf16[128,6144]{1,0:T(8,128)(2,1)S(1)} %constant_dynamic-update-slice_fusion.refs_0_), channel_id=1, source_target_pairs={{0,24},{1,97},{2,26},{3,99},{4,28},{5,101},{6,30},{7,103},{8,0},{9... | collective-permute-start | bytes 4718600 | tf_op jit(solution)/shard_map/ppermute | solution.py:24
  47.1 25.2 %collective-permute-start.21 = (bf16[64,6144]{1,0:T(8,128)(2,1)S(1)}, bf16[64,6144]{1,0:T(8,128)(2,1)S(1)}, u32[]{:S(2)}, u32[]{:S(2)}) collective-permute-start(bf16[64,6144]{1,0:T(8,128)(2,1)S(1)} %slice.76), channel_id=1, source_target_pairs={{0,8},{1,33},{2,10},{3,35},{4,12},{5,37},{6,14},{7,39},{8,16},{9,4... | collective-permute-start | bytes 2359304 | tf_op jit(solution)/shard_map/ppermute | solution.py:24
  47.7 25.1 %collective-permute-start.23 = (bf16[64,6144]{1,0:T(8,128)(2,1)S(1)}, bf16[64,6144]{1,0:T(8,128)(2,1)S(1)}, u32[]{:S(2)}, u32[]{:S(2)}) collective-permute-start(bf16[64,6144]{1,0:T(8,128)(2,1)S(1)} %slice.77), channel_id=1, source_target_pairs={{0,24},{1,97},{2,26},{3,99},{4,28},{5,101},{6,30},{7,103},{8,0},{9... | collective-permute-start | bytes 2359304 | tf_op jit(solution)/shard_map/ppermute | solution.py:24
  64.0 16.8 %collective-permute-start.18 = (bf16[64,6144]{1,0:T(8,128)(2,1)S(1)}, bf16[64,6144]{1,0:T(8,128)(2,1)S(1)}, u32[]{:S(2)}, u32[]{:S(2)}) collective-permute-start(bf16[64,6144]{1,0:T(8,128)(2,1)S(1)} %slice.74), channel_id=1, source_target_pairs={{0,8},{1,33},{2,10},{3,35},{4,12},{5,37},{6,14},{7,39},{8,16},{9,4... | collective-permute-start | bytes 2359304 | tf_op jit(solution)/shard_map/ppermute | solution.py:24
  64.6 16.7 %collective-permute-start.20 = (bf16[64,6144]{1,0:T(8,128)(2,1)S(1)}, bf16[64,6144]{1,0:T(8,128)(2,1)S(1)}, u32[]{:S(2)}, u32[]{:S(2)}) collective-permute-start(bf16[64,6144]{1,0:T(8,128)(2,1)S(1)} %slice.75), channel_id=1, source_target_pairs={{0,24},{1,97},{2,26},{3,99},{4,28},{5,101},{6,30},{7,103},{8,0},{9... | collective-permute-start | bytes 2359304 | tf_op jit(solution)/shard_map/ppermute | solution.py:24
  72.3 8.9 %collective-permute-start.22 = (bf16[64,6144]{1,0:T(8,128)(2,1)S(1)}, bf16[64,6144]{1,0:T(8,128)(2,1)S(1)}, u32[]{:S(2)}, u32[]{:S(2)}) collective-permute-start(bf16[64,6144]{1,0:T(8,128)(2,1)S(1)} %collective-permute-done.21), channel_id=1, source_target_pairs={{0,1},{1,0},{2,3},{3,2},{4,5},{5,4},{6,7},{7,6},{8,9},{9,8},{10,11... | collective-permute-start | bytes 2359304 | tf_op jit(solution)/shard_map/ppermute | solution.py:24
  72.8 8.4 %collective-permute-start.24 = (bf16[64,6144]{1,0:T(8,128)(2,1)S(1)}, bf16[64,6144]{1,0:T(8,128)(2,1)S(1)}, u32[]{:S(2)}, u32[]{:S(2)}) collective-permute-start(bf16[64,6144]{1,0:T(8,128)(2,1)S(1)} %collective-permute-done.23), channel_id=1, source_target_pairs={{0,1},{1,0},{2,3},{3,2},{4,5},{5,4},{6,7},{7,6},{8,9},{9,8},{10,11... | collective-permute-start | bytes 2359304 | tf_op jit(solution)/shard_map/ppermute | solution.py:24
  92.3 12.3 %collective-permute-start.40 = (bf16[64,6144]{1,0:T(8,128)(2,1)S(1)}, bf16[64,6144]{1,0:T(8,128)(2,1)S(1)}, u32[]{:S(2)}, u32[]{:S(2)}) collective-permute-start(bf16[64,6144]{1,0:T(8,128)(2,1)S(1)} %get-tuple-element.53), channel_id=1, source_target_pairs={{0,24},{1,97},{2,26},{3,99},{4,28},{5,101},{6,30},{7,103},{8,0},{9... | collective-permute-start | bytes 2359304 | tf_op jit(solution)/shard_map/ppermute | solution.py:24
  95.1 12.0 %collective-permute-start.8 = (bf16[128,6144]{1,0:T(8,128)(2,1)S(1)}, bf16[128,6144]{1,0:T(8,128)(2,1)S(1)}, u32[]{:S(2)}, u32[]{:S(2)}) collective-permute-start(bf16[128,6144]{1,0:T(8,128)(2,1)S(1)} %constant_dynamic-update-slice_fusion.5), channel_id=1, source_target_pairs={{0,1},{1,0},{2,3},{3,2},{4,5},{5,4},{6,7},{7,6},{8,9},{9,8},{10,11... | collective-permute-start | bytes 4718600 | tf_op jit(solution)/shard_map/ppermute | solution.py:24
  102.6 35.5 %collective-permute-start.39 = (bf16[64,6144]{1,0:T(8,128)(2,1)S(1)}, bf16[64,6144]{1,0:T(8,128)(2,1)S(1)}, u32[]{:S(2)}, u32[]{:S(2)}) collective-permute-start(bf16[64,6144]{1,0:T(8,128)(2,1)S(1)} %get-tuple-element.51), channel_id=1, source_target_pairs={{0,8},{1,33},{2,10},{3,35},{4,12},{5,37},{6,14},{7,39},{8,16},{9,4... | collective-permute-start | bytes 2359304 | tf_op jit(solution)/shard_map/ppermute | solution.py:24
  102.6 22.7 %collective-permute-start.11 = (bf16[128,6144]{1,0:T(8,128)(2,1)S(1)}, bf16[128,6144]{1,0:T(8,128)(2,1)S(1)}, u32[]{:S(2)}, u32[]{:S(2)}) collective-permute-start(bf16[128,6144]{1,0:T(8,128)(2,1)S(1)} %collective-permute-done.10), channel_id=1, source_target_pairs={{0,1},{1,0},{2,3},{3,2},{4,5},{5,4},{6,7},{7,6},{8,9},{9,8},{10,11... | collective-permute-start | bytes 4718600 | tf_op jit(solution)/shard_map/ppermute | solution.py:24
  103.6 22.2 %collective-permute-start.13 = (bf16[128,6144]{1,0:T(8,128)(2,1)S(1)}, bf16[128,6144]{1,0:T(8,128)(2,1)S(1)}, u32[]{:S(2)}, u32[]{:S(2)}) collective-permute-start(bf16[128,6144]{1,0:T(8,128)(2,1)S(1)} %collective-permute-done.12), channel_id=1, source_target_pairs={{0,1},{1,0},{2,3},{3,2},{4,5},{5,4},{6,7},{7,6},{8,9},{9,8},{10,11... | collective-permute-start | bytes 4718600 | tf_op jit(solution)/shard_map/ppermute | solution.py:24
  104.6 19.7 %collective-permute-start.43 = (bf16[64,6144]{1,0:T(8,128)(2,1)S(1)}, bf16[64,6144]{1,0:T(8,128)(2,1)S(1)}, u32[]{:S(2)}, u32[]{:S(2)}) collective-permute-start(bf16[64,6144]{1,0:T(8,128)(2,1)S(1)} %get-tuple-element.57), channel_id=1, source_target_pairs={{0,8},{1,33},{2,10},{3,35},{4,12},{5,37},{6,14},{7,39},{8,16},{9,4... | collective-permute-start | bytes 2359304 | tf_op jit(solution)/shard_map/ppermute | solution.py:24
  107.0 33.5 %collective-permute-start.42 = (bf16[64,6144]{1,0:T(8,128)(2,1)S(1)}, bf16[64,6144]{1,0:T(8,128)(2,1)S(1)}, u32[]{:S(2)}, u32[]{:S(2)}) collective-permute-start(bf16[64,6144]{1,0:T(8,128)(2,1)S(1)} %get-tuple-element.55), channel_id=1, source_target_pairs={{0,24},{1,97},{2,26},{3,99},{4,28},{5,101},{6,30},{7,103},{8,0},{9... | collective-permute-start | bytes 2359304 | tf_op jit(solution)/shard_map/ppermute | solution.py:24
  124.3 17.1 %collective-permute-start.25 = (bf16[64,6144]{1,0:T(8,128)(2,1)S(1)}, bf16[64,6144]{1,0:T(8,128)(2,1)}, u32[]{:S(2)}, u32[]{:S(2)}) collective-permute-start(bf16[64,6144]{1,0:T(8,128)(2,1)S(1)} %get-tuple-element.40), channel_id=1, source_target_pairs={{0,1},{1,0},{2,3},{3,2},{4,5},{5,4},{6,7},{7,6},{8,9},{9,8},{10,11... | collective-permute-start | bytes 2359304 | tf_op jit(solution)/shard_map/ppermute | solution.py:24
  125.3 32.5 %collective-permute-start.41 = (bf16[64,6144]{1,0:T(8,128)(2,1)}, bf16[64,6144]{1,0:T(8,128)(2,1)}, u32[]{:S(2)}, u32[]{:S(2)}) collective-permute-start(bf16[64,6144]{1,0:T(8,128)(2,1)} %add_convert_fusion.1), channel_id=1, source_target_pairs={{0,24},{1,97},{2,26},{3,99},{4,28},{5,101},{6,30},{7,103},{8,0},{9... | collective-permute-start | bytes 2359304 | tf_op jit(solution)/shard_map/ppermute | solution.py:24
  125.8 34.8 %collective-permute-start.44 = (bf16[64,6144]{1,0:T(8,128)(2,1)}, bf16[64,6144]{1,0:T(8,128)(2,1)}, u32[]{:S(2)}, u32[]{:S(2)}) collective-permute-start(bf16[64,6144]{1,0:T(8,128)(2,1)} %add_convert_fusion), channel_id=1, source_target_pairs={{0,8},{1,33},{2,10},{3,35},{4,12},{5,37},{6,14},{7,39},{8,16},{9,4... | collective-permute-start | bytes 2359304 | tf_op jit(solution)/shard_map/ppermute | solution.py:24
  139.0 23.8 %collective-permute-start.16 = (bf16[64,6144]{1,0:T(8,128)(2,1)}, bf16[64,6144]{1,0:T(8,128)(2,1)}, u32[]{:S(2)}, u32[]{:S(2)}) collective-permute-start(bf16[64,6144]{1,0:T(8,128)(2,1)} %get-tuple-element.39), channel_id=1, source_target_pairs={{0,1},{1,0},{2,3},{3,2},{4,5},{5,4},{6,7},{7,6},{8,9},{9,8},{10,11... | collective-permute-start | bytes 2359304 | tf_op jit(solution)/shard_map/ppermute | solution.py:24
  141.4 21.9 %collective-permute-start.32 = (bf16[64,6144]{1,0:T(8,128)(2,1)}, bf16[64,6144]{1,0:T(8,128)(2,1)}, u32[]{:S(2)}, u32[]{:S(2)}) collective-permute-start(bf16[64,6144]{1,0:T(8,128)(2,1)} %get-tuple-element.44), channel_id=1, source_target_pairs={{0,1},{1,0},{2,3},{3,2},{4,5},{5,4},{6,7},{7,6},{8,9},{9,8},{10,11... | collective-permute-start | bytes 2359304 | tf_op jit(solution)/shard_map/ppermute | solution.py:24
  141.4 22.0 %collective-permute-start.26 = (bf16[64,6144]{1,0:T(8,128)(2,1)}, bf16[64,6144]{1,0:T(8,128)(2,1)}, u32[]{:S(2)}, u32[]{:S(2)}) collective-permute-start(bf16[64,6144]{1,0:T(8,128)(2,1)} %collective-permute-done.25), channel_id=1, source_target_pairs={{0,24},{1,97},{2,26},{3,99},{4,28},{5,101},{6,30},{7,103},{8,0},{9... | collective-permute-start | bytes 2359304 | tf_op jit(solution)/shard_map/ppermute | solution.py:24
  157.9 19.9 %collective-permute-start.9 = (bf16[64,6144]{1,0:T(8,128)(2,1)S(1)}, bf16[64,6144]{1,0:T(8,128)(2,1)S(1)}, u32[]{:S(2)}, u32[]{:S(2)}) collective-permute-start(bf16[64,6144]{1,0:T(8,128)(2,1)S(1)} %get-tuple-element.37), channel_id=1, source_target_pairs={{0,1},{1,0},{2,3},{3,2},{4,5},{5,4},{6,7},{7,6},{8,9},{9,8},{10,11... | collective-permute-start | bytes 2359304 | tf_op jit(solution)/shard_map/ppermute | solution.py:24
  163.4 13.4 %collective-permute-start.33 = (bf16[64,6144]{1,0:T(8,128)(2,1)}, bf16[64,6144]{1,0:T(8,128)(2,1)S(1)}, u32[]{:S(2)}, u32[]{:S(2)}) collective-permute-start(bf16[64,6144]{1,0:T(8,128)(2,1)} %collective-permute-done.32), channel_id=1, source_target_pairs={{0,8},{1,33},{2,10},{3,35},{4,12},{5,37},{6,14},{7,39},{8,16},{9,4... | collective-permute-start | bytes 2359304 | tf_op jit(solution)/shard_map/ppermute | solution.py:24
  164.9 12.9 %collective-permute-start.28 = (bf16[64,6144]{1,0:T(8,128)(2,1)S(1)}, bf16[64,6144]{1,0:T(8,128)(2,1)S(1)}, u32[]{:S(2)}, u32[]{:S(2)}) collective-permute-start(bf16[64,6144]{1,0:T(8,128)(2,1)S(1)} %get-tuple-element.41), channel_id=1, source_target_pairs={{0,1},{1,0},{2,3},{3,2},{4,5},{5,4},{6,7},{7,6},{8,9},{9,8},{10,11... | collective-permute-start | bytes 2359304 | tf_op jit(solution)/shard_map/ppermute | solution.py:24
  165.4 23.4 %collective-permute-start.15 = (bf16[64,6144]{1,0:T(8,128)(2,1)S(1)}, bf16[64,6144]{1,0:T(8,128)(2,1)S(1)}, u32[]{:S(2)}, u32[]{:S(2)}) collective-permute-start(bf16[64,6144]{1,0:T(8,128)(2,1)S(1)} %collective-permute-done.14), channel_id=1, source_target_pairs={{0,8},{1,33},{2,10},{3,35},{4,12},{5,37},{6,14},{7,39},{8,16},{9,4... | collective-permute-start | bytes 2359304 | tf_op jit(solution)/shard_map/ppermute | solution.py:24
  166.3 25.8 %collective-permute-start.30 = (bf16[64,6144]{1,0:T(8,128)(2,1)S(1)}, bf16[64,6144]{1,0:T(8,128)(2,1)S(1)}, u32[]{:S(2)}, u32[]{:S(2)}) collective-permute-start(bf16[64,6144]{1,0:T(8,128)(2,1)S(1)} %collective-permute-done.29), channel_id=1, source_target_pairs={{0,24},{1,97},{2,26},{3,99},{4,28},{5,101},{6,30},{7,103},{8,0},{9... | collective-permute-start | bytes 2359304 | tf_op jit(solution)/shard_map/ppermute | solution.py:24
  176.8 12.0 %collective-permute-start.45 = (bf16[32,6144]{1,0:T(8,128)(2,1)S(1)}, bf16[32,6144]{1,0:T(8,128)(2,1)S(1)}, u32[]{:S(2)}, u32[]{:S(2)}) collective-permute-start(bf16[32,6144]{1,0:T(8,128)(2,1)S(1)} %get-tuple-element.59), channel_id=1, source_target_pairs={{0,96},{1,25},{2,98},{3,27},{4,100},{5,29},{6,102},{7,31},{8,104},... | collective-permute-start | bytes 1179656 | tf_op jit(solution)/shard_map/ppermute | solution.py:24
  177.8 15.9 %collective-permute-start.27 = (bf16[64,6144]{1,0:T(8,128)(2,1)S(1)}, bf16[64,6144]{1,0:T(8,128)(2,1)S(1)}, u32[]{:S(2)}, u32[]{:S(2)}) collective-permute-start(bf16[64,6144]{1,0:T(8,128)(2,1)S(1)} %add_convert_fusion.3), channel_id=1, source_target_pairs={{0,24},{1,97},{2,26},{3,99},{4,28},{5,101},{6,30},{7,103},{8,0},{9... | collective-permute-start | bytes 2359304 | tf_op jit(solution)/shard_map/ppermute | solution.py:24
  177.9 19.6 %collective-permute-start.34 = (bf16[64,6144]{1,0:T(8,128)(2,1)S(1)}, bf16[64,6144]{1,0:T(8,128)(2,1)S(1)}, u32[]{:S(2)}, u32[]{:S(2)}) collective-permute-start(bf16[64,6144]{1,0:T(8,128)(2,1)S(1)} %add_convert_fusion.2), channel_id=1, source_target_pairs={{0,8},{1,33},{2,10},{3,35},{4,12},{5,37},{6,14},{7,39},{8,16},{9,4... | collective-permute-start | bytes 2359304 | tf_op jit(solution)/shard_map/ppermute | solution.py:24
  188.8 9.9 %collective-permute-start.46 = (bf16[32,6144]{1,0:T(8,128)(2,1)S(1)}, bf16[32,6144]{1,0:T(8,128)(2,1)S(1)}, u32[]{:S(2)}, u32[]{:S(2)}) collective-permute-start(bf16[32,6144]{1,0:T(8,128)(2,1)S(1)} %get-tuple-element.60), channel_id=1, source_target_pairs={{0,32},{1,9},{2,34},{3,11},{4,36},{5,13},{6,38},{7,15},{8,40},{9,1... | collective-permute-start | bytes 1179656 | tf_op jit(solution)/shard_map/ppermute | solution.py:24
  188.8 21.8 %collective-permute-start.47 = (bf16[16,6144]{1,0:T(8,128)(2,1)S(1)}, bf16[16,6144]{1,0:T(8,128)(2,1)S(1)}, u32[]{:S(2)}, u32[]{:S(2)}) collective-permute-start(bf16[16,6144]{1,0:T(8,128)(2,1)S(1)} %add_convert_fusion.5), channel_id=1, source_target_pairs={{0,96},{1,25},{2,98},{3,27},{4,100},{5,29},{6,102},{7,31},{8,104},... | collective-permute-start | bytes 589832 | tf_op jit(solution)/shard_map/ppermute | solution.py:24
  198.1 7.8 %collective-permute-start.35 = (bf16[32,6144]{1,0:T(8,128)(2,1)S(1)}, bf16[32,6144]{1,0:T(8,128)(2,1)S(1)}, u32[]{:S(2)}, u32[]{:S(2)}) collective-permute-start(bf16[32,6144]{1,0:T(8,128)(2,1)S(1)} %get-tuple-element.46), channel_id=1, source_target_pairs={{0,96},{1,25},{2,98},{3,27},{4,100},{5,29},{6,102},{7,31},{8,104},... | collective-permute-start | bytes 1179656 | tf_op jit(solution)/shard_map/ppermute | solution.py:24
  198.7 11.9 %collective-permute-start.48 = (bf16[16,6144]{1,0:T(8,128)(2,1)S(1)}, bf16[16,6144]{1,0:T(8,128)(2,1)S(1)}, u32[]{:S(2)}, u32[]{:S(2)}) collective-permute-start(bf16[16,6144]{1,0:T(8,128)(2,1)S(1)} %add_convert_fusion.4), channel_id=1, source_target_pairs={{0,32},{1,9},{2,34},{3,11},{4,36},{5,13},{6,38},{7,15},{8,40},{9,1... | collective-permute-start | bytes 589832 | tf_op jit(solution)/shard_map/ppermute | solution.py:24
  200.5 9.6 %collective-permute-start.36 = (bf16[32,6144]{1,0:T(8,128)(2,1)S(1)}, bf16[32,6144]{1,0:T(8,128)(2,1)S(1)}, u32[]{:S(2)}, u32[]{:S(2)}) collective-permute-start(bf16[32,6144]{1,0:T(8,128)(2,1)S(1)} %get-tuple-element.47), channel_id=1, source_target_pairs={{0,32},{1,9},{2,34},{3,11},{4,36},{5,13},{6,38},{7,15},{8,40},{9,1... | collective-permute-start | bytes 1179656 | tf_op jit(solution)/shard_map/ppermute | solution.py:24
  210.1 6.9 %collective-permute-start.38 = (bf16[16,6144]{1,0:T(8,128)(2,1)S(1)}, bf16[16,6144]{1,0:T(8,128)(2,1)S(1)}, u32[]{:S(2)}, u32[]{:S(2)}) collective-permute-start(bf16[16,6144]{1,0:T(8,128)(2,1)S(1)} %add_convert_fusion.6), channel_id=1, source_target_pairs={{0,32},{1,9},{2,34},{3,11},{4,36},{5,13},{6,38},{7,15},{8,40},{9,1... | collective-permute-start | bytes 589832 | tf_op jit(solution)/shard_map/ppermute | solution.py:24
  220.9 9.8 %collective-permute-start.50 = (bf16[128,768]{1,0:T(8,128)(2,1)S(1)}, bf16[128,768]{1,0:T(8,128)(2,1)S(1)}, u32[]{:S(2)}, u32[]{:S(2)}) collective-permute-start(bf16[128,768]{1,0:T(8,128)(2,1)S(1)} %get-tuple-element.66), channel_id=1, source_target_pairs={{0,4},{1,5},{2,6},{3,7},{4,0},{5,1},{6,2},{7,3},{8,12},{9,13},{10,... | collective-permute-start | bytes 589832 | tf_op jit(solution)/shard_map/ppermute | solution.py:24
  224.9 9.4 %collective-permute-start.51 = (bf16[128,768]{1,0:T(8,128)(2,1)S(1)}, bf16[128,768]{1,0:T(8,128)(2,1)S(1)}, u32[]{:S(2)}, u32[]{:S(2)}) collective-permute-start(bf16[128,768]{1,0:T(8,128)(2,1)S(1)} %get-tuple-element.67), channel_id=1, source_target_pairs={{0,2},{1,3},{2,4},{3,5},{4,6},{5,7},{6,0},{7,1},{8,10},{9,11},{10,... | collective-permute-start | bytes 589832 | tf_op jit(solution)/shard_map/ppermute | solution.py:24
  225.9 9.1 %collective-permute-start.52 = (bf16[128,768]{1,0:T(8,128)(2,1)S(1)}, bf16[128,768]{1,0:T(8,128)(2,1)S(1)}, u32[]{:S(2)}, u32[]{:S(2)}) collective-permute-start(bf16[128,768]{1,0:T(8,128)(2,1)S(1)} %get-tuple-element.68), channel_id=1, source_target_pairs={{0,6},{1,7},{2,0},{3,1},{4,2},{5,3},{6,4},{7,5},{8,14},{9,15},{10,... | collective-permute-start | bytes 589832 | tf_op jit(solution)/shard_map/ppermute | solution.py:24
  (26 other events, 312.0 us)

commit v3 on v2

--- a/solution.py
+++ b/solution.py
@@ -222,8 +222,10 @@
         member = jnp.any(matched, axis=-1).astype(jnp.int32)
         weight = jnp.sum(jnp.where(matched, gates, 0.0), axis=-1)
         position = jnp.cumsum(member) - member
-        limit = jnp.sum(jnp.where(jnp.arange(experts, dtype=jnp.int32) == expert, capacity, 0))
-        kept = (member == 1) & (position < limit)
+        ids = jnp.arange(experts, dtype=jnp.int32)
+        named = (routes[:, :, None] == ids) & (ids == expert)
+        limit = jnp.sum(jnp.where(named, capacity, 0), axis=(1, 2))
+        kept = position < limit
         picked = kept[None, :] & (position[None, :] == slot_ids[:, None])
         return picked.astype(BF16), weight
 

time: 236 us -> 234 us (level)
  no operation moved by 1% of the time
where the time goes in v3:
time: 234 us
  waiting for transfers between devices  110 us (47%)
  starting transfers between devices  62.7 us (27%)
  Pallas kernels  36.7 us (16%)
  local copies, waits for them, and re-layouts  16.5 us (7%)
  other arithmetic  6.65 us (3%)
    ppermute x53, waiting for transfers between devices, move(): return lax.ppermute(value, ('dp', 'expert'), pairs)  110 us
    ppermute x53, starting transfers between devices, move(): return lax.ppermute(value, ('dp', 'expert'), pairs)  62.7 us
    pallas_call x4, Pallas kernels, ffn(): pl.pallas_call(lambda *refs: ffn_kernel(len(sizes), *refs), name='ffn', g...  31.3 us
    unnamed x48, local copies, waits for them, and re-layouts  15.8 us
    pallas_call x5, Pallas kernels, vmem_call(): pl.pallas_call(kernel, in_specs=specs, out_specs=[space] * len(outs), out...  5.42 us
  transfers between devices with their start and end apart: 53, of which 24 were waited for; matrix products, arithmetic and copies ran while one was open for 2% of the time, Pallas kernels for 11%

profile of v3, /device:TPU:0, one launch (start us, length us, event | category | flops | bytes accessed | tf_op | source)
XLA Modules:
  0.0 233.9 jit_solution(9964338704394555096)
XLA Ops:
  3.1 1.7 collective-permute-start
  4.8 1.6 collective-permute-start.1
  6.8 2.8 %collective-permute-start.5 = (bf16[32,6144]{1,0:T(8,128)(2,1)S(1)}, bf16[32,6144]{1,0:T(8,128)(2,1)S(1)}, u32[]{:S(2)}, u32[]{:S(2)}) collective-permute-start(bf16[32,6144]{1,0:T(8,128)(2,1)S(1)} %get-tuple-element.79), channel_id=1, source_target_pairs={{0,96},{1,25},{2,98},{3,27},{4,100},{5,29},{6,102},{7,31},{8,104},... | collective-permute-start | bytes 1179656 | tf_op jit(solution)/shard_map/ppermute | solution.py:24
  9.6 2.5 %collective-permute-done = bf16[32,6144]{1,0:T(8,128)(2,1)S(1)} collective-permute-done((bf16[32,6144]{1,0:T(8,128)(2,1)S(1)}, bf16[32,6144]{1,0:T(8,128)(2,1)S(1)}, u32[]{:S(2)}, u32[]{:S(2)}) %collective-permute-start) | collective-permute-done | bytes 393248 | tf_op jit(solution)/shard_map/ppermute | solution.py:24
  12.7 2.9 %collective-permute-start.3 = (bf16[16,6144]{1,0:T(8,128)(2,1)S(1)}, bf16[16,6144]{1,0:T(8,128)(2,1)S(1)}, u32[]{:S(2)}, u32[]{:S(2)}) collective-permute-start(bf16[16,6144]{1,0:T(8,128)(2,1)S(1)} %slice.70), channel_id=1, source_target_pairs={{0,96},{1,25},{2,98},{3,27},{4,100},{5,29},{6,102},{7,31},{8,104},... | collective-permute-start | bytes 589832 | tf_op jit(solution)/shard_map/ppermute | solution.py:24
  16.9 2.9 %collective-permute-start.7 = (bf16[16,6144]{1,0:T(8,128)(2,1)S(1)}, bf16[16,6144]{1,0:T(8,128)(2,1)S(1)}, u32[]{:S(2)}, u32[]{:S(2)}) collective-permute-start(bf16[16,6144]{1,0:T(8,128)(2,1)S(1)} %slice.73), channel_id=1, source_target_pairs={{0,96},{1,25},{2,98},{3,27},{4,100},{5,29},{6,102},{7,31},{8,104},... | collective-permute-start | bytes 589832 | tf_op jit(solution)/shard_map/ppermute | solution.py:24
  19.9 3.4 %collective-permute-done.6 = bf16[16,6144]{1,0:T(8,128)(2,1)S(1)} collective-permute-done((bf16[16,6144]{1,0:T(8,128)(2,1)S(1)}, bf16[16,6144]{1,0:T(8,128)(2,1)S(1)}, u32[]{:S(2)}, u32[]{:S(2)}) %collective-permute-start.6) | collective-permute-done | bytes 196640 | tf_op jit(solution)/shard_map/ppermute | solution.py:24
  23.4 1.8 collective-permute-start.10
  25.2 1.5 collective-permute-start.12
  27.3 2.7 %collective-permute-start.19 = (bf16[128,6144]{1,0:T(8,128)(2,1)S(1)}, bf16[128,6144]{1,0:T(8,128)(2,1)S(1)}, u32[]{:S(2)}, u32[]{:S(2)}) collective-permute-start(bf16[128,6144]{1,0:T(8,128)(2,1)S(1)} %constant_dynamic-update-slice_fusion.refs_0_), channel_id=1, source_target_pairs={{0,24},{1,97},{2,26},{3,99},{4,28},{5,101},{6,30},{7,103},{8,0},{9... | collective-permute-start | bytes 4718600 | tf_op jit(solution)/shard_map/ppermute | solution.py:24
  30.1 15.0 %collective-permute-done.10 = bf16[128,6144]{1,0:T(8,128)(2,1)S(1)} collective-permute-done((bf16[128,6144]{1,0:T(8,128)(2,1)S(1)}, bf16[128,6144]{1,0:T(8,128)(2,1)S(1)}, u32[]{:S(2)}, u32[]{:S(2)}) %collective-permute-start.10) | collective-permute-done | bytes 1572896 | tf_op jit(solution)/shard_map/ppermute | solution.py:24
  45.8 2.8 %collective-permute-start.23 = (bf16[64,6144]{1,0:T(8,128)(2,1)S(1)}, bf16[64,6144]{1,0:T(8,128)(2,1)S(1)}, u32[]{:S(2)}, u32[]{:S(2)}) collective-permute-start(bf16[64,6144]{1,0:T(8,128)(2,1)S(1)} %slice.77), channel_id=1, source_target_pairs={{0,24},{1,97},{2,26},{3,99},{4,28},{5,101},{6,30},{7,103},{8,0},{9... | collective-permute-start | bytes 2359304 | tf_op jit(solution)/shard_map/ppermute | solution.py:24
  48.6 13.4 %collective-permute-done.17.refs_0_ = bf16[128,6144]{1,0:T(8,128)(2,1)S(1)} collective-permute-done((bf16[128,6144]{1,0:T(8,128)(2,1)S(1)}, bf16[128,6144]{1,0:T(8,128)(2,1)S(1)}, u32[]{:S(2)}, u32[]{:S(2)}) %collective-permute-start.17) | collective-permute-done | bytes 1572896 | tf_op jit(solution)/shard_map/ppermute | solution.py:24
  62.6 2.8 %collective-permute-start.20 = (bf16[64,6144]{1,0:T(8,128)(2,1)S(1)}, bf16[64,6144]{1,0:T(8,128)(2,1)S(1)}, u32[]{:S(2)}, u32[]{:S(2)}) collective-permute-start(bf16[64,6144]{1,0:T(8,128)(2,1)S(1)} %slice.75), channel_id=1, source_target_pairs={{0,24},{1,97},{2,26},{3,99},{4,28},{5,101},{6,30},{7,103},{8,0},{9... | collective-permute-start | bytes 2359304 | tf_op jit(solution)/shard_map/ppermute | solution.py:24
  65.4 4.9 %collective-permute-done.21 = bf16[64,6144]{1,0:T(8,128)(2,1)S(1)} collective-permute-done((bf16[64,6144]{1,0:T(8,128)(2,1)S(1)}, bf16[64,6144]{1,0:T(8,128)(2,1)S(1)}, u32[]{:S(2)}, u32[]{:S(2)}) %collective-permute-start.21) | collective-permute-done | bytes 786464 | tf_op jit(solution)/shard_map/ppermute | solution.py:24
  70.9 7.9 %collective-permute-done.18.refs_0_ = bf16[64,6144]{1,0:T(8,128)(2,1)S(1)} collective-permute-done((bf16[64,6144]{1,0:T(8,128)(2,1)S(1)}, bf16[64,6144]{1,0:T(8,128)(2,1)S(1)}, u32[]{:S(2)}, u32[]{:S(2)}) %collective-permute-start.18) | collective-permute-done | bytes 786464 | tf_op jit(solution)/shard_map/ppermute | solution.py:24
  79.3 2.8 %copy-done.5 = bf16[1,512,6144]{2,1,0:T(8,128)(2,1)S(1)} copy-done((bf16[1,512,6144]{2,1,0:T(8,128)(2,1)S(1)}, bf16[1,512,6144]{2,1,0:T(8,128)(2,1)}, u32[]{:S(2)}) %copy-start.5) | copy-done | bytes 6291480
  82.1 8.2 %ffn.6 = (bf16[64,6144]{1,0:T(8,128)(2,1)S(1)}, bf16[64,6144]{1,0:T(8,128)(2,1)S(1)}, bf16[64,6144]{1,0:T(8,128)(2,1)S(1)}, bf16[64,6144]{1,0:T(8,128)(2,1)}) custom-call(bf16[64,6144]{1,0:T(8,128)(2,1)S(1)} %collective-permute-done.18.refs_0_, bf16[64,6144]{1,0:T(8,128)(2,1)S(1)} %collective-permute-done.20.refs_1_, ...), custom_call_target="tpu_custom_call" | custom-call | flops 4831838208 | bytes 25165824 | tf_op jit(solution)/shard_map/ffn/pallas_call | solution.py:188
  90.4 2.7 %collective-permute-start.40 = (bf16[64,6144]{1,0:T(8,128)(2,1)S(1)}, bf16[64,6144]{1,0:T(8,128)(2,1)S(1)}, u32[]{:S(2)}, u32[]{:S(2)}) collective-permute-start(bf16[64,6144]{1,0:T(8,128)(2,1)S(1)} %get-tuple-element.53), channel_id=1, source_target_pairs={{0,24},{1,97},{2,26},{3,99},{4,28},{5,101},{6,30},{7,103},{8,0},{9... | collective-permute-start | bytes 2359304 | tf_op jit(solution)/shard_map/ppermute | solution.py:24
  93.1 7.5 %ffn.7 = (bf16[64,6144]{1,0:T(8,128)(2,1)S(1)}, bf16[64,6144]{1,0:T(8,128)(2,1)S(1)}, bf16[64,6144]{1,0:T(8,128)(2,1)S(1)}, bf16[64,6144]{1,0:T(8,128)(2,1)S(1)}) custom-call(bf16[128,6144]{1,0:T(8,128)(2,1)S(1)} %collective-permute-done.17.refs_0_, bf16[128,6144]{1,0:T(8,128)(2,1)S(1)} %collective-permute-done.19.refs_1_, ...), custom_call_target="tpu_custom_call" | custom-call | flops 4831838208 | bytes 25165824 | tf_op jit(solution)/shard_map/ffn/pallas_call | solution.py:188
  105.1 2.4 %collective-permute-start.42 = (bf16[64,6144]{1,0:T(8,128)(2,1)S(1)}, bf16[64,6144]{1,0:T(8,128)(2,1)S(1)}, u32[]{:S(2)}, u32[]{:S(2)}) collective-permute-start(bf16[64,6144]{1,0:T(8,128)(2,1)S(1)} %get-tuple-element.55), channel_id=1, source_target_pairs={{0,24},{1,97},{2,26},{3,99},{4,28},{5,101},{6,30},{7,103},{8,0},{9... | collective-permute-start | bytes 2359304 | tf_op jit(solution)/shard_map/ppermute | solution.py:24
  107.5 14.8 %collective-permute-done.43 = bf16[64,6144]{1,0:T(8,128)(2,1)S(1)} collective-permute-done((bf16[64,6144]{1,0:T(8,128)(2,1)S(1)}, bf16[64,6144]{1,0:T(8,128)(2,1)S(1)}, u32[]{:S(2)}, u32[]{:S(2)}) %collective-permute-start.43) | collective-permute-done | bytes 786464 | tf_op jit(solution)/shard_map/ppermute | solution.py:24
  123.8 1.6 collective-permute-start.44
  125.4 8.0 %ffn.5 = (bf16[64,6144]{1,0:T(8,128)(2,1)}, bf16[64,6144]{1,0:T(8,128)(2,1)S(1)}, bf16[64,6144]{1,0:T(8,128)(2,1)S(1)}, bf16[64,6144]{1,0:T(8,128)(2,1)S(1)}) custom-call(bf16[128,6144]{1,0:T(8,128)(2,1)S(1)} %collective-permute-done.11.refs_0_, bf16[128,6144]{1,0:T(8,128)(2,1)S(1)} %collective-permute-done.13.refs_1_, bf16[1,6144,512]{2,1,0:T(8,128)(2,1)S(1)} %bitcast.11, ...), custom_call_target="tpu_custom_call" | custom-call | flops 4831838208 | bytes 25165824 | tf_op jit(solution)/shard_map/ffn/pallas_call | solution.py:188
  137.0 1.5 collective-permute-start.16
  140.0 2.8 %copy-done.2 = bf16[1,6144,512]{2,1,0:T(8,128)(2,1)S(1)} copy-done((bf16[1,6144,512]{2,1,0:T(8,128)(2,1)S(1)}, bf16[1,6144,512]{2,1,0:T(8,128)(2,1)}, u32[]{:S(2)}) %copy-start.2) | copy-done | bytes 6291480
  142.8 2.8 %copy-done.4 = bf16[1,6144,512]{2,1,0:T(8,128)(2,1)S(1)} copy-done((bf16[1,6144,512]{2,1,0:T(8,128)(2,1)S(1)}, bf16[1,6144,512]{2,1,0:T(8,128)(2,1)}, u32[]{:S(2)}) %copy-start.4) | copy-done | bytes 6291480
  145.6 2.8 %copy-done.6 = bf16[1,512,6144]{2,1,0:T(8,128)(2,1)S(1)} copy-done((bf16[1,512,6144]{2,1,0:T(8,128)(2,1)S(1)}, bf16[1,512,6144]{2,1,0:T(8,128)(2,1)}, u32[]{:S(2)}) %copy-start.6) | copy-done | bytes 6291480
  148.4 7.5 %ffn.4 = (bf16[64,6144]{1,0:T(8,128)(2,1)S(1)}, bf16[64,6144]{1,0:T(8,128)(2,1)S(1)}, bf16[64,6144]{1,0:T(8,128)(2,1)S(1)}, bf16[64,6144]{1,0:T(8,128)(2,1)S(1)}) custom-call(bf16[128,6144]{1,0:T(8,128)(2,1)S(1)} %constant_dynamic-update-slice_fusion.refs_0_, bf16[128,6144]{1,0:T(8,128)(2,1)S(1)} %collective-permute-done.8.refs_1_, ...), custom_call_target="tpu_custom_call" | custom-call | flops 4831838208 | bytes 25165824 | tf_op jit(solution)/shard_map/ffn/pallas_call | solution.py:188
  155.9 2.6 %collective-permute-start.9 = (bf16[64,6144]{1,0:T(8,128)(2,1)S(1)}, bf16[64,6144]{1,0:T(8,128)(2,1)S(1)}, u32[]{:S(2)}, u32[]{:S(2)}) collective-permute-start(bf16[64,6144]{1,0:T(8,128)(2,1)S(1)} %get-tuple-element.37), channel_id=1, source_target_pairs={{0,1},{1,0},{2,3},{3,2},{4,5},{5,4},{6,7},{7,6},{8,9},{9,8},{10,11... | collective-permute-start | bytes 2359304 | tf_op jit(solution)/shard_map/ppermute | solution.py:24
  158.6 2.1 shard_map.74
  161.3 1.6 add_convert_fusion.3
  164.3 2.4 %collective-permute-start.30 = (bf16[64,6144]{1,0:T(8,128)(2,1)S(1)}, bf16[64,6144]{1,0:T(8,128)(2,1)S(1)}, u32[]{:S(2)}, u32[]{:S(2)}) collective-permute-start(bf16[64,6144]{1,0:T(8,128)(2,1)S(1)} %collective-permute-done.29), channel_id=1, source_target_pairs={{0,24},{1,97},{2,26},{3,99},{4,28},{5,101},{6,30},{7,103},{8,0},{9... | collective-permute-start | bytes 2359304 | tf_op jit(solution)/shard_map/ppermute | solution.py:24
  166.6 8.1 %collective-permute-done.33 = bf16[64,6144]{1,0:T(8,128)(2,1)S(1)} collective-permute-done((bf16[64,6144]{1,0:T(8,128)(2,1)}, bf16[64,6144]{1,0:T(8,128)(2,1)S(1)}, u32[]{:S(2)}, u32[]{:S(2)}) %collective-permute-start.33) | collective-permute-done | bytes 786464 | tf_op jit(solution)/shard_map/ppermute | solution.py:24
  175.9 2.0 collective-permute-start.34
  177.9 8.9 %collective-permute-done.45.refs_6_ = bf16[32,6144]{1,0:T(8,128)(2,1)S(1)} collective-permute-done((bf16[32,6144]{1,0:T(8,128)(2,1)S(1)}, bf16[32,6144]{1,0:T(8,128)(2,1)S(1)}, u32[]{:S(2)}, u32[]{:S(2)}) %collective-permute-start.45) | collective-permute-done | bytes 393248 | tf_op jit(solution)/shard_map/ppermute | solution.py:24
  186.8 3.3 %collective-permute-start.47 = (bf16[16,6144]{1,0:T(8,128)(2,1)S(1)}, bf16[16,6144]{1,0:T(8,128)(2,1)S(1)}, u32[]{:S(2)}, u32[]{:S(2)}) collective-permute-start(bf16[16,6144]{1,0:T(8,128)(2,1)S(1)} %add_convert_fusion.5), channel_id=1, source_target_pairs={{0,96},{1,25},{2,98},{3,27},{4,100},{5,29},{6,102},{7,31},{8,104},... | collective-permute-start | bytes 589832 | tf_op jit(solution)/shard_map/ppermute | solution.py:24
  190.1 1.5 collective-permute-done.27.from_after
  191.6 3.8 %collective-permute-done.34.from_before = bf16[64,6144]{1,0:T(8,128)(2,1)S(1)} collective-permute-done((bf16[64,6144]{1,0:T(8,128)(2,1)S(1)}, bf16[64,6144]{1,0:T(8,128)(2,1)S(1)}, u32[]{:S(2)}, u32[]{:S(2)}) %collective-permute-start.34) | collective-permute-done | bytes 786464 | tf_op jit(solution)/shard_map/ppermute | solution.py:24
  196.7 1.8 collective-permute-start.48
  198.6 5.3 %collective-permute-done.35.refs_1_ = bf16[32,6144]{1,0:T(8,128)(2,1)S(1)} collective-permute-done((bf16[32,6144]{1,0:T(8,128)(2,1)S(1)}, bf16[32,6144]{1,0:T(8,128)(2,1)S(1)}, u32[]{:S(2)}, u32[]{:S(2)}) %collective-permute-start.35) | collective-permute-done | bytes 393248 | tf_op jit(solution)/shard_map/ppermute | solution.py:24
  204.0 1.8 collective-permute-start.37
  205.8 2.3 collective-permute-done.36.refs_2_
  209.7 5.4 %collective-permute-done.38.refs_4_ = bf16[16,6144]{1,0:T(8,128)(2,1)S(1)} collective-permute-done((bf16[16,6144]{1,0:T(8,128)(2,1)S(1)}, bf16[16,6144]{1,0:T(8,128)(2,1)S(1)}, u32[]{:S(2)}, u32[]{:S(2)}) %collective-permute-start.38) | collective-permute-done | bytes 196640 | tf_op jit(solution)/shard_map/ppermute | solution.py:24
  218.8 4.1 %collective-permute-start.50 = (bf16[128,768]{1,0:T(8,128)(2,1)S(1)}, bf16[128,768]{1,0:T(8,128)(2,1)S(1)}, u32[]{:S(2)}, u32[]{:S(2)}) collective-permute-start(bf16[128,768]{1,0:T(8,128)(2,1)S(1)} %get-tuple-element.66), channel_id=1, source_target_pairs={{0,4},{1,5},{2,6},{3,7},{4,0},{5,1},{6,2},{7,3},{8,12},{9,13},{10,... | collective-permute-start | bytes 589832 | tf_op jit(solution)/shard_map/ppermute | solution.py:24
  224.0 2.2 collective-permute-start.52
  226.2 2.5 %collective-permute-done.50.refs_0_ = bf16[128,768]{1,0:T(8,128)(2,1)S(1)} collective-permute-done((bf16[128,768]{1,0:T(8,128)(2,1)S(1)}, bf16[128,768]{1,0:T(8,128)(2,1)S(1)}, u32[]{:S(2)}, u32[]{:S(2)}) %collective-permute-start.50) | collective-permute-done | bytes 196640 | tf_op jit(solution)/shard_map/ppermute | solution.py:24
  228.7 3.7 %collective-permute-done.51.refs_1_ = bf16[128,768]{1,0:T(8,128)(2,1)S(1)} collective-permute-done((bf16[128,768]{1,0:T(8,128)(2,1)S(1)}, bf16[128,768]{1,0:T(8,128)(2,1)S(1)}, u32[]{:S(2)}, u32[]{:S(2)}) %collective-permute-start.51) | collective-permute-done | bytes 196640 | tf_op jit(solution)/shard_map/ppermute | solution.py:24
  (157 shorter events, 31.9 us)
Async XLA Ops:
  3.1 9.1 %collective-permute-start = (bf16[32,6144]{1,0:T(8,128)(2,1)S(1)}, bf16[32,6144]{1,0:T(8,128)(2,1)S(1)}, u32[]{:S(2)}, u32[]{:S(2)}) collective-permute-start(bf16[32,6144]{1,0:T(8,128)(2,1)S(1)} %get-tuple-element.82), channel_id=1, source_target_pairs={{0,32},{1,9},{2,34},{3,11},{4,36},{5,13},{6,38},{7,15},{8,40},{9,1... | collective-permute-start | bytes 1179656 | tf_op jit(solution)/shard_map/ppermute | solution.py:24
  4.8 7.9 %collective-permute-start.1 = (bf16[32,6144]{1,0:T(8,128)(2,1)S(1)}, bf16[32,6144]{1,0:T(8,128)(2,1)S(1)}, u32[]{:S(2)}, u32[]{:S(2)}) collective-permute-start(bf16[32,6144]{1,0:T(8,128)(2,1)S(1)} %get-tuple-element.82), channel_id=1, source_target_pairs={{0,96},{1,25},{2,98},{3,27},{4,100},{5,29},{6,102},{7,31},{8,104},... | collective-permute-start | bytes 1179656 | tf_op jit(solution)/shard_map/ppermute | solution.py:24
  6.4 10.0 %collective-permute-start.4 = (bf16[32,6144]{1,0:T(8,128)(2,1)S(1)}, bf16[32,6144]{1,0:T(8,128)(2,1)S(1)}, u32[]{:S(2)}, u32[]{:S(2)}) collective-permute-start(bf16[32,6144]{1,0:T(8,128)(2,1)S(1)} %get-tuple-element.79), channel_id=1, source_target_pairs={{0,32},{1,9},{2,34},{3,11},{4,36},{5,13},{6,38},{7,15},{8,40},{9,1... | collective-permute-start | bytes 1179656 | tf_op jit(solution)/shard_map/ppermute | solution.py:24
  6.8 10.1 %collective-permute-start.5 = (bf16[32,6144]{1,0:T(8,128)(2,1)S(1)}, bf16[32,6144]{1,0:T(8,128)(2,1)S(1)}, u32[]{:S(2)}, u32[]{:S(2)}) collective-permute-start(bf16[32,6144]{1,0:T(8,128)(2,1)S(1)} %get-tuple-element.79), channel_id=1, source_target_pairs={{0,96},{1,25},{2,98},{3,27},{4,100},{5,29},{6,102},{7,31},{8,104},... | collective-permute-start | bytes 1179656 | tf_op jit(solution)/shard_map/ppermute | solution.py:24
  12.2 14.5 %collective-permute-start.2 = (bf16[16,6144]{1,0:T(8,128)(2,1)S(1)}, bf16[16,6144]{1,0:T(8,128)(2,1)S(1)}, u32[]{:S(2)}, u32[]{:S(2)}) collective-permute-start(bf16[16,6144]{1,0:T(8,128)(2,1)S(1)} %slice.69), channel_id=1, source_target_pairs={{0,32},{1,9},{2,34},{3,11},{4,36},{5,13},{6,38},{7,15},{8,40},{9,1... | collective-permute-start | bytes 589832 | tf_op jit(solution)/shard_map/ppermute | solution.py:24
  12.7 14.0 %collective-permute-start.3 = (bf16[16,6144]{1,0:T(8,128)(2,1)S(1)}, bf16[16,6144]{1,0:T(8,128)(2,1)S(1)}, u32[]{:S(2)}, u32[]{:S(2)}) collective-permute-start(bf16[16,6144]{1,0:T(8,128)(2,1)S(1)} %slice.70), channel_id=1, source_target_pairs={{0,96},{1,25},{2,98},{3,27},{4,100},{5,29},{6,102},{7,31},{8,104},... | collective-permute-start | bytes 589832 | tf_op jit(solution)/shard_map/ppermute | solution.py:24
  16.4 6.9 %collective-permute-start.6 = (bf16[16,6144]{1,0:T(8,128)(2,1)S(1)}, bf16[16,6144]{1,0:T(8,128)(2,1)S(1)}, u32[]{:S(2)}, u32[]{:S(2)}) collective-permute-start(bf16[16,6144]{1,0:T(8,128)(2,1)S(1)} %slice.72), channel_id=1, source_target_pairs={{0,32},{1,9},{2,34},{3,11},{4,36},{5,13},{6,38},{7,15},{8,40},{9,1... | collective-permute-start | bytes 589832 | tf_op jit(solution)/shard_map/ppermute | solution.py:24
  16.9 6.5 %collective-permute-start.7 = (bf16[16,6144]{1,0:T(8,128)(2,1)S(1)}, bf16[16,6144]{1,0:T(8,128)(2,1)S(1)}, u32[]{:S(2)}, u32[]{:S(2)}) collective-permute-start(bf16[16,6144]{1,0:T(8,128)(2,1)S(1)} %slice.73), channel_id=1, source_target_pairs={{0,96},{1,25},{2,98},{3,27},{4,100},{5,29},{6,102},{7,31},{8,104},... | collective-permute-start | bytes 589832 | tf_op jit(solution)/shard_map/ppermute | solution.py:24
  23.4 21.7 %collective-permute-start.10 = (bf16[128,6144]{1,0:T(8,128)(2,1)S(1)}, bf16[128,6144]{1,0:T(8,128)(2,1)S(1)}, u32[]{:S(2)}, u32[]{:S(2)}) collective-permute-start(bf16[128,6144]{1,0:T(8,128)(2,1)S(1)} %constant_dynamic-update-slice_fusion.5), channel_id=1, source_target_pairs={{0,8},{1,33},{2,10},{3,35},{4,12},{5,37},{6,14},{7,39},{8,16},{9,4... | collective-permute-start | bytes 4718600 | tf_op jit(solution)/shard_map/ppermute | solution.py:24
  25.2 20.5 %collective-permute-start.12 = (bf16[128,6144]{1,0:T(8,128)(2,1)S(1)}, bf16[128,6144]{1,0:T(8,128)(2,1)S(1)}, u32[]{:S(2)}, u32[]{:S(2)}) collective-permute-start(bf16[128,6144]{1,0:T(8,128)(2,1)S(1)} %constant_dynamic-update-slice_fusion.5), channel_id=1, source_target_pairs={{0,24},{1,97},{2,26},{3,99},{4,28},{5,101},{6,30},{7,103},{8,0},{9... | collective-permute-start | bytes 4718600 | tf_op jit(solution)/shard_map/ppermute | solution.py:24
  26.7 35.2 %collective-permute-start.17 = (bf16[128,6144]{1,0:T(8,128)(2,1)S(1)}, bf16[128,6144]{1,0:T(8,128)(2,1)S(1)}, u32[]{:S(2)}, u32[]{:S(2)}) collective-permute-start(bf16[128,6144]{1,0:T(8,128)(2,1)S(1)} %constant_dynamic-update-slice_fusion.refs_0_), channel_id=1, source_target_pairs={{0,8},{1,33},{2,10},{3,35},{4,12},{5,37},{6,14},{7,39},{8,16},{9,4... | collective-permute-start | bytes 4718600 | tf_op jit(solution)/shard_map/ppermute | solution.py:24
  27.3 35.2 %collective-permute-start.19 = (bf16[128,6144]{1,0:T(8,128)(2,1)S(1)}, bf16[128,6144]{1,0:T(8,128)(2,1)S(1)}, u32[]{:S(2)}, u32[]{:S(2)}) collective-permute-start(bf16[128,6144]{1,0:T(8,128)(2,1)S(1)} %constant_dynamic-update-slice_fusion.refs_0_), channel_id=1, source_target_pairs={{0,24},{1,97},{2,26},{3,99},{4,28},{5,101},{6,30},{7,103},{8,0},{9... | collective-permute-start | bytes 4718600 | tf_op jit(solution)/shard_map/ppermute | solution.py:24
  45.1 25.2 %collective-permute-start.21 = (bf16[64,6144]{1,0:T(8,128)(2,1)S(1)}, bf16[64,6144]{1,0:T(8,128)(2,1)S(1)}, u32[]{:S(2)}, u32[]{:S(2)}) collective-permute-start(bf16[64,6144]{1,0:T(8,128)(2,1)S(1)} %slice.76), channel_id=1, source_target_pairs={{0,8},{1,33},{2,10},{3,35},{4,12},{5,37},{6,14},{7,39},{8,16},{9,4... | collective-permute-start | bytes 2359304 | tf_op jit(solution)/shard_map/ppermute | solution.py:24
  45.8 25.1 %collective-permute-start.23 = (bf16[64,6144]{1,0:T(8,128)(2,1)S(1)}, bf16[64,6144]{1,0:T(8,128)(2,1)S(1)}, u32[]{:S(2)}, u32[]{:S(2)}) collective-permute-start(bf16[64,6144]{1,0:T(8,128)(2,1)S(1)} %slice.77), channel_id=1, source_target_pairs={{0,24},{1,97},{2,26},{3,99},{4,28},{5,101},{6,30},{7,103},{8,0},{9... | collective-permute-start | bytes 2359304 | tf_op jit(solution)/shard_map/ppermute | solution.py:24
  62.0 16.8 %collective-permute-start.18 = (bf16[64,6144]{1,0:T(8,128)(2,1)S(1)}, bf16[64,6144]{1,0:T(8,128)(2,1)S(1)}, u32[]{:S(2)}, u32[]{:S(2)}) collective-permute-start(bf16[64,6144]{1,0:T(8,128)(2,1)S(1)} %slice.74), channel_id=1, source_target_pairs={{0,8},{1,33},{2,10},{3,35},{4,12},{5,37},{6,14},{7,39},{8,16},{9,4... | collective-permute-start | bytes 2359304 | tf_op jit(solution)/shard_map/ppermute | solution.py:24
  62.6 16.7 %collective-permute-start.20 = (bf16[64,6144]{1,0:T(8,128)(2,1)S(1)}, bf16[64,6144]{1,0:T(8,128)(2,1)S(1)}, u32[]{:S(2)}, u32[]{:S(2)}) collective-permute-start(bf16[64,6144]{1,0:T(8,128)(2,1)S(1)} %slice.75), channel_id=1, source_target_pairs={{0,24},{1,97},{2,26},{3,99},{4,28},{5,101},{6,30},{7,103},{8,0},{9... | collective-permute-start | bytes 2359304 | tf_op jit(solution)/shard_map/ppermute | solution.py:24
  70.4 8.9 %collective-permute-start.22 = (bf16[64,6144]{1,0:T(8,128)(2,1)S(1)}, bf16[64,6144]{1,0:T(8,128)(2,1)S(1)}, u32[]{:S(2)}, u32[]{:S(2)}) collective-permute-start(bf16[64,6144]{1,0:T(8,128)(2,1)S(1)} %collective-permute-done.21), channel_id=1, source_target_pairs={{0,1},{1,0},{2,3},{3,2},{4,5},{5,4},{6,7},{7,6},{8,9},{9,8},{10,11... | collective-permute-start | bytes 2359304 | tf_op jit(solution)/shard_map/ppermute | solution.py:24
  70.9 8.4 %collective-permute-start.24 = (bf16[64,6144]{1,0:T(8,128)(2,1)S(1)}, bf16[64,6144]{1,0:T(8,128)(2,1)S(1)}, u32[]{:S(2)}, u32[]{:S(2)}) collective-permute-start(bf16[64,6144]{1,0:T(8,128)(2,1)S(1)} %collective-permute-done.23), channel_id=1, source_target_pairs={{0,1},{1,0},{2,3},{3,2},{4,5},{5,4},{6,7},{7,6},{8,9},{9,8},{10,11... | collective-permute-start | bytes 2359304 | tf_op jit(solution)/shard_map/ppermute | solution.py:24
  90.4 12.2 %collective-permute-start.40 = (bf16[64,6144]{1,0:T(8,128)(2,1)S(1)}, bf16[64,6144]{1,0:T(8,128)(2,1)S(1)}, u32[]{:S(2)}, u32[]{:S(2)}) collective-permute-start(bf16[64,6144]{1,0:T(8,128)(2,1)S(1)} %get-tuple-element.53), channel_id=1, source_target_pairs={{0,24},{1,97},{2,26},{3,99},{4,28},{5,101},{6,30},{7,103},{8,0},{9... | collective-permute-start | bytes 2359304 | tf_op jit(solution)/shard_map/ppermute | solution.py:24
  93.1 12.0 %collective-permute-start.8 = (bf16[128,6144]{1,0:T(8,128)(2,1)S(1)}, bf16[128,6144]{1,0:T(8,128)(2,1)S(1)}, u32[]{:S(2)}, u32[]{:S(2)}) collective-permute-start(bf16[128,6144]{1,0:T(8,128)(2,1)S(1)} %constant_dynamic-update-slice_fusion.5), channel_id=1, source_target_pairs={{0,1},{1,0},{2,3},{3,2},{4,5},{5,4},{6,7},{7,6},{8,9},{9,8},{10,11... | collective-permute-start | bytes 4718600 | tf_op jit(solution)/shard_map/ppermute | solution.py:24
  100.6 35.5 %collective-permute-start.39 = (bf16[64,6144]{1,0:T(8,128)(2,1)S(1)}, bf16[64,6144]{1,0:T(8,128)(2,1)S(1)}, u32[]{:S(2)}, u32[]{:S(2)}) collective-permute-start(bf16[64,6144]{1,0:T(8,128)(2,1)S(1)} %get-tuple-element.51), channel_id=1, source_target_pairs={{0,8},{1,33},{2,10},{3,35},{4,12},{5,37},{6,14},{7,39},{8,16},{9,4... | collective-permute-start | bytes 2359304 | tf_op jit(solution)/shard_map/ppermute | solution.py:24
  100.7 22.7 %collective-permute-start.11 = (bf16[128,6144]{1,0:T(8,128)(2,1)S(1)}, bf16[128,6144]{1,0:T(8,128)(2,1)S(1)}, u32[]{:S(2)}, u32[]{:S(2)}) collective-permute-start(bf16[128,6144]{1,0:T(8,128)(2,1)S(1)} %collective-permute-done.10), channel_id=1, source_target_pairs={{0,1},{1,0},{2,3},{3,2},{4,5},{5,4},{6,7},{7,6},{8,9},{9,8},{10,11... | collective-permute-start | bytes 4718600 | tf_op jit(solution)/shard_map/ppermute | solution.py:24
  101.6 22.2 %collective-permute-start.13 = (bf16[128,6144]{1,0:T(8,128)(2,1)S(1)}, bf16[128,6144]{1,0:T(8,128)(2,1)S(1)}, u32[]{:S(2)}, u32[]{:S(2)}) collective-permute-start(bf16[128,6144]{1,0:T(8,128)(2,1)S(1)} %collective-permute-done.12), channel_id=1, source_target_pairs={{0,1},{1,0},{2,3},{3,2},{4,5},{5,4},{6,7},{7,6},{8,9},{9,8},{10,11... | collective-permute-start | bytes 4718600 | tf_op jit(solution)/shard_map/ppermute | solution.py:24
  102.6 19.7 %collective-permute-start.43 = (bf16[64,6144]{1,0:T(8,128)(2,1)S(1)}, bf16[64,6144]{1,0:T(8,128)(2,1)S(1)}, u32[]{:S(2)}, u32[]{:S(2)}) collective-permute-start(bf16[64,6144]{1,0:T(8,128)(2,1)S(1)} %get-tuple-element.57), channel_id=1, source_target_pairs={{0,8},{1,33},{2,10},{3,35},{4,12},{5,37},{6,14},{7,39},{8,16},{9,4... | collective-permute-start | bytes 2359304 | tf_op jit(solution)/shard_map/ppermute | solution.py:24
  105.1 33.4 %collective-permute-start.42 = (bf16[64,6144]{1,0:T(8,128)(2,1)S(1)}, bf16[64,6144]{1,0:T(8,128)(2,1)S(1)}, u32[]{:S(2)}, u32[]{:S(2)}) collective-permute-start(bf16[64,6144]{1,0:T(8,128)(2,1)S(1)} %get-tuple-element.55), channel_id=1, source_target_pairs={{0,24},{1,97},{2,26},{3,99},{4,28},{5,101},{6,30},{7,103},{8,0},{9... | collective-permute-start | bytes 2359304 | tf_op jit(solution)/shard_map/ppermute | solution.py:24
  122.3 17.1 %collective-permute-start.25 = (bf16[64,6144]{1,0:T(8,128)(2,1)S(1)}, bf16[64,6144]{1,0:T(8,128)(2,1)}, u32[]{:S(2)}, u32[]{:S(2)}) collective-permute-start(bf16[64,6144]{1,0:T(8,128)(2,1)S(1)} %get-tuple-element.40), channel_id=1, source_target_pairs={{0,1},{1,0},{2,3},{3,2},{4,5},{5,4},{6,7},{7,6},{8,9},{9,8},{10,11... | collective-permute-start | bytes 2359304 | tf_op jit(solution)/shard_map/ppermute | solution.py:24
  123.4 32.5 %collective-permute-start.41 = (bf16[64,6144]{1,0:T(8,128)(2,1)}, bf16[64,6144]{1,0:T(8,128)(2,1)}, u32[]{:S(2)}, u32[]{:S(2)}) collective-permute-start(bf16[64,6144]{1,0:T(8,128)(2,1)} %add_convert_fusion.1), channel_id=1, source_target_pairs={{0,24},{1,97},{2,26},{3,99},{4,28},{5,101},{6,30},{7,103},{8,0},{9... | collective-permute-start | bytes 2359304 | tf_op jit(solution)/shard_map/ppermute | solution.py:24
  123.8 34.7 %collective-permute-start.44 = (bf16[64,6144]{1,0:T(8,128)(2,1)}, bf16[64,6144]{1,0:T(8,128)(2,1)}, u32[]{:S(2)}, u32[]{:S(2)}) collective-permute-start(bf16[64,6144]{1,0:T(8,128)(2,1)} %add_convert_fusion), channel_id=1, source_target_pairs={{0,8},{1,33},{2,10},{3,35},{4,12},{5,37},{6,14},{7,39},{8,16},{9,4... | collective-permute-start | bytes 2359304 | tf_op jit(solution)/shard_map/ppermute | solution.py:24
  137.0 23.8 %collective-permute-start.16 = (bf16[64,6144]{1,0:T(8,128)(2,1)}, bf16[64,6144]{1,0:T(8,128)(2,1)}, u32[]{:S(2)}, u32[]{:S(2)}) collective-permute-start(bf16[64,6144]{1,0:T(8,128)(2,1)} %get-tuple-element.39), channel_id=1, source_target_pairs={{0,1},{1,0},{2,3},{3,2},{4,5},{5,4},{6,7},{7,6},{8,9},{9,8},{10,11... | collective-permute-start | bytes 2359304 | tf_op jit(solution)/shard_map/ppermute | solution.py:24
  139.4 21.9 %collective-permute-start.32 = (bf16[64,6144]{1,0:T(8,128)(2,1)}, bf16[64,6144]{1,0:T(8,128)(2,1)}, u32[]{:S(2)}, u32[]{:S(2)}) collective-permute-start(bf16[64,6144]{1,0:T(8,128)(2,1)} %get-tuple-element.44), channel_id=1, source_target_pairs={{0,1},{1,0},{2,3},{3,2},{4,5},{5,4},{6,7},{7,6},{8,9},{9,8},{10,11... | collective-permute-start | bytes 2359304 | tf_op jit(solution)/shard_map/ppermute | solution.py:24
  139.4 22.0 %collective-permute-start.26 = (bf16[64,6144]{1,0:T(8,128)(2,1)}, bf16[64,6144]{1,0:T(8,128)(2,1)}, u32[]{:S(2)}, u32[]{:S(2)}) collective-permute-start(bf16[64,6144]{1,0:T(8,128)(2,1)} %collective-permute-done.25), channel_id=1, source_target_pairs={{0,24},{1,97},{2,26},{3,99},{4,28},{5,101},{6,30},{7,103},{8,0},{9... | collective-permute-start | bytes 2359304 | tf_op jit(solution)/shard_map/ppermute | solution.py:24
  155.9 19.9 %collective-permute-start.9 = (bf16[64,6144]{1,0:T(8,128)(2,1)S(1)}, bf16[64,6144]{1,0:T(8,128)(2,1)S(1)}, u32[]{:S(2)}, u32[]{:S(2)}) collective-permute-start(bf16[64,6144]{1,0:T(8,128)(2,1)S(1)} %get-tuple-element.37), channel_id=1, source_target_pairs={{0,1},{1,0},{2,3},{3,2},{4,5},{5,4},{6,7},{7,6},{8,9},{9,8},{10,11... | collective-permute-start | bytes 2359304 | tf_op jit(solution)/shard_map/ppermute | solution.py:24
  161.3 13.4 %collective-permute-start.33 = (bf16[64,6144]{1,0:T(8,128)(2,1)}, bf16[64,6144]{1,0:T(8,128)(2,1)S(1)}, u32[]{:S(2)}, u32[]{:S(2)}) collective-permute-start(bf16[64,6144]{1,0:T(8,128)(2,1)} %collective-permute-done.32), channel_id=1, source_target_pairs={{0,8},{1,33},{2,10},{3,35},{4,12},{5,37},{6,14},{7,39},{8,16},{9,4... | collective-permute-start | bytes 2359304 | tf_op jit(solution)/shard_map/ppermute | solution.py:24
  162.9 12.9 %collective-permute-start.28 = (bf16[64,6144]{1,0:T(8,128)(2,1)S(1)}, bf16[64,6144]{1,0:T(8,128)(2,1)S(1)}, u32[]{:S(2)}, u32[]{:S(2)}) collective-permute-start(bf16[64,6144]{1,0:T(8,128)(2,1)S(1)} %get-tuple-element.41), channel_id=1, source_target_pairs={{0,1},{1,0},{2,3},{3,2},{4,5},{5,4},{6,7},{7,6},{8,9},{9,8},{10,11... | collective-permute-start | bytes 2359304 | tf_op jit(solution)/shard_map/ppermute | solution.py:24
  163.4 23.4 %collective-permute-start.15 = (bf16[64,6144]{1,0:T(8,128)(2,1)S(1)}, bf16[64,6144]{1,0:T(8,128)(2,1)S(1)}, u32[]{:S(2)}, u32[]{:S(2)}) collective-permute-start(bf16[64,6144]{1,0:T(8,128)(2,1)S(1)} %collective-permute-done.14), channel_id=1, source_target_pairs={{0,8},{1,33},{2,10},{3,35},{4,12},{5,37},{6,14},{7,39},{8,16},{9,4... | collective-permute-start | bytes 2359304 | tf_op jit(solution)/shard_map/ppermute | solution.py:24
  164.3 25.8 %collective-permute-start.30 = (bf16[64,6144]{1,0:T(8,128)(2,1)S(1)}, bf16[64,6144]{1,0:T(8,128)(2,1)S(1)}, u32[]{:S(2)}, u32[]{:S(2)}) collective-permute-start(bf16[64,6144]{1,0:T(8,128)(2,1)S(1)} %collective-permute-done.29), channel_id=1, source_target_pairs={{0,24},{1,97},{2,26},{3,99},{4,28},{5,101},{6,30},{7,103},{8,0},{9... | collective-permute-start | bytes 2359304 | tf_op jit(solution)/shard_map/ppermute | solution.py:24
  174.8 12.0 %collective-permute-start.45 = (bf16[32,6144]{1,0:T(8,128)(2,1)S(1)}, bf16[32,6144]{1,0:T(8,128)(2,1)S(1)}, u32[]{:S(2)}, u32[]{:S(2)}) collective-permute-start(bf16[32,6144]{1,0:T(8,128)(2,1)S(1)} %get-tuple-element.59), channel_id=1, source_target_pairs={{0,96},{1,25},{2,98},{3,27},{4,100},{5,29},{6,102},{7,31},{8,104},... | collective-permute-start | bytes 1179656 | tf_op jit(solution)/shard_map/ppermute | solution.py:24
  175.8 15.9 %collective-permute-start.27 = (bf16[64,6144]{1,0:T(8,128)(2,1)S(1)}, bf16[64,6144]{1,0:T(8,128)(2,1)S(1)}, u32[]{:S(2)}, u32[]{:S(2)}) collective-permute-start(bf16[64,6144]{1,0:T(8,128)(2,1)S(1)} %add_convert_fusion.3), channel_id=1, source_target_pairs={{0,24},{1,97},{2,26},{3,99},{4,28},{5,101},{6,30},{7,103},{8,0},{9... | collective-permute-start | bytes 2359304 | tf_op jit(solution)/shard_map/ppermute | solution.py:24
  175.9 19.6 %collective-permute-start.34 = (bf16[64,6144]{1,0:T(8,128)(2,1)S(1)}, bf16[64,6144]{1,0:T(8,128)(2,1)S(1)}, u32[]{:S(2)}, u32[]{:S(2)}) collective-permute-start(bf16[64,6144]{1,0:T(8,128)(2,1)S(1)} %add_convert_fusion.2), channel_id=1, source_target_pairs={{0,8},{1,33},{2,10},{3,35},{4,12},{5,37},{6,14},{7,39},{8,16},{9,4... | collective-permute-start | bytes 2359304 | tf_op jit(solution)/shard_map/ppermute | solution.py:24
  186.7 9.9 %collective-permute-start.46 = (bf16[32,6144]{1,0:T(8,128)(2,1)S(1)}, bf16[32,6144]{1,0:T(8,128)(2,1)S(1)}, u32[]{:S(2)}, u32[]{:S(2)}) collective-permute-start(bf16[32,6144]{1,0:T(8,128)(2,1)S(1)} %get-tuple-element.60), channel_id=1, source_target_pairs={{0,32},{1,9},{2,34},{3,11},{4,36},{5,13},{6,38},{7,15},{8,40},{9,1... | collective-permute-start | bytes 1179656 | tf_op jit(solution)/shard_map/ppermute | solution.py:24
  186.8 21.8 %collective-permute-start.47 = (bf16[16,6144]{1,0:T(8,128)(2,1)S(1)}, bf16[16,6144]{1,0:T(8,128)(2,1)S(1)}, u32[]{:S(2)}, u32[]{:S(2)}) collective-permute-start(bf16[16,6144]{1,0:T(8,128)(2,1)S(1)} %add_convert_fusion.5), channel_id=1, source_target_pairs={{0,96},{1,25},{2,98},{3,27},{4,100},{5,29},{6,102},{7,31},{8,104},... | collective-permute-start | bytes 589832 | tf_op jit(solution)/shard_map/ppermute | solution.py:24
  196.1 7.8 %collective-permute-start.35 = (bf16[32,6144]{1,0:T(8,128)(2,1)S(1)}, bf16[32,6144]{1,0:T(8,128)(2,1)S(1)}, u32[]{:S(2)}, u32[]{:S(2)}) collective-permute-start(bf16[32,6144]{1,0:T(8,128)(2,1)S(1)} %get-tuple-element.46), channel_id=1, source_target_pairs={{0,96},{1,25},{2,98},{3,27},{4,100},{5,29},{6,102},{7,31},{8,104},... | collective-permute-start | bytes 1179656 | tf_op jit(solution)/shard_map/ppermute | solution.py:24
  196.7 11.9 %collective-permute-start.48 = (bf16[16,6144]{1,0:T(8,128)(2,1)S(1)}, bf16[16,6144]{1,0:T(8,128)(2,1)S(1)}, u32[]{:S(2)}, u32[]{:S(2)}) collective-permute-start(bf16[16,6144]{1,0:T(8,128)(2,1)S(1)} %add_convert_fusion.4), channel_id=1, source_target_pairs={{0,32},{1,9},{2,34},{3,11},{4,36},{5,13},{6,38},{7,15},{8,40},{9,1... | collective-permute-start | bytes 589832 | tf_op jit(solution)/shard_map/ppermute | solution.py:24
  198.5 9.6 %collective-permute-start.36 = (bf16[32,6144]{1,0:T(8,128)(2,1)S(1)}, bf16[32,6144]{1,0:T(8,128)(2,1)S(1)}, u32[]{:S(2)}, u32[]{:S(2)}) collective-permute-start(bf16[32,6144]{1,0:T(8,128)(2,1)S(1)} %get-tuple-element.47), channel_id=1, source_target_pairs={{0,32},{1,9},{2,34},{3,11},{4,36},{5,13},{6,38},{7,15},{8,40},{9,1... | collective-permute-start | bytes 1179656 | tf_op jit(solution)/shard_map/ppermute | solution.py:24
  208.1 6.9 %collective-permute-start.38 = (bf16[16,6144]{1,0:T(8,128)(2,1)S(1)}, bf16[16,6144]{1,0:T(8,128)(2,1)S(1)}, u32[]{:S(2)}, u32[]{:S(2)}) collective-permute-start(bf16[16,6144]{1,0:T(8,128)(2,1)S(1)} %add_convert_fusion.6), channel_id=1, source_target_pairs={{0,32},{1,9},{2,34},{3,11},{4,36},{5,13},{6,38},{7,15},{8,40},{9,1... | collective-permute-start | bytes 589832 | tf_op jit(solution)/shard_map/ppermute | solution.py:24
  218.8 9.8 %collective-permute-start.50 = (bf16[128,768]{1,0:T(8,128)(2,1)S(1)}, bf16[128,768]{1,0:T(8,128)(2,1)S(1)}, u32[]{:S(2)}, u32[]{:S(2)}) collective-permute-start(bf16[128,768]{1,0:T(8,128)(2,1)S(1)} %get-tuple-element.66), channel_id=1, source_target_pairs={{0,4},{1,5},{2,6},{3,7},{4,0},{5,1},{6,2},{7,3},{8,12},{9,13},{10,... | collective-permute-start | bytes 589832 | tf_op jit(solution)/shard_map/ppermute | solution.py:24
  222.9 9.4 %collective-permute-start.51 = (bf16[128,768]{1,0:T(8,128)(2,1)S(1)}, bf16[128,768]{1,0:T(8,128)(2,1)S(1)}, u32[]{:S(2)}, u32[]{:S(2)}) collective-permute-start(bf16[128,768]{1,0:T(8,128)(2,1)S(1)} %get-tuple-element.67), channel_id=1, source_target_pairs={{0,2},{1,3},{2,4},{3,5},{4,6},{5,7},{6,0},{7,1},{8,10},{9,11},{10,... | collective-permute-start | bytes 589832 | tf_op jit(solution)/shard_map/ppermute | solution.py:24
  224.0 9.1 %collective-permute-start.52 = (bf16[128,768]{1,0:T(8,128)(2,1)S(1)}, bf16[128,768]{1,0:T(8,128)(2,1)S(1)}, u32[]{:S(2)}, u32[]{:S(2)}) collective-permute-start(bf16[128,768]{1,0:T(8,128)(2,1)S(1)} %get-tuple-element.68), channel_id=1, source_target_pairs={{0,6},{1,7},{2,0},{3,1},{4,2},{5,3},{6,4},{7,5},{8,14},{9,15},{10,... | collective-permute-start | bytes 589832 | tf_op jit(solution)/shard_map/ppermute | solution.py:24
  (26 other events, 310.1 us)
